TPU v7x, 32 devices: a whole 2x2x4 slice. The times are simulated.
32 devices in a mesh: order: 16 (over z, x, core), slab: 2 (over y).
Axes of the slice: x: 2, y: 2, z: 4, core: 2. Of those that a mesh axis runs over, the one named last changes fastest.
Arguments:
- direct: float32 [16, 2, 256, 1024], P('order', None, 'slab'), may hold values from -6 to 6
- adjoint: float32 [16, 2, 256, 1024], P('order', None, 'slab'), may hold values from -6 to 6
- sound: float32 [256, 1024], P('slab'), may hold values from 0.5 to 4
- transverse: float32 [1024, 1024], replicated, may hold values from -0.1875 to 0.1875
- burner_temp: float32 [16], replicated, may hold values from -4 to 4
- burner_gain: float32 [16], replicated, may hold values from -4 to 4
- flame_cells: int32 [4096], replicated, may hold values from 0 to 262143
- flame_weight: float32 [4096], replicated, may hold values from 0.5 to 4
- offsets: int32 [4], replicated, may hold values from 1 to 15
Outputs:
- image: float32 [16, 2, 256, 1024], P('order', None, 'slab')
- coupling: float32 [16, 2, 4], P('order')
All inputs are finite; a program needn't handle non-finite values.
Results may differ from a plain program's by a relative error of at most 0.0003.
Values sent between devices are 32-bit elements; how exact they have to be, the bound alone decides.
No kernel may reach another device: no remote copies, remote signals or barrier semaphores. Data moves between devices by JAX's collectives and lax.ppermute only.
A program may use at most 128 MiB of HBM per device.

v0:
```python
import functools
import math

import jax
import jax.numpy as jnp
from jax import lax
from jax.experimental import pallas as pl
from jax.experimental.pallas import tpu as pltpu
from jax.sharding import PartitionSpec as P


VMEM = pltpu.VMEM
SMEM = pltpu.SMEM
LANES = 128
LATE = 2
BARE = 2
LAST = 2
LIMIT = 20 * 1024 * 1024


def first_kernel(half, rows, partners, direct_ref, sound_ref, *refs):
    body_refs = refs[: len(partners)]
    top_ref, bottom_ref, *block_refs, sems = refs[len(partners) :]
    layers, width = sound_ref.shape
    mid = width // 2
    here = lax.axis_index("order") % half
    copies = []

    def begin(source, target):
        copies.append(pltpu.make_async_copy(source, target, sems.at[len(copies)]))
        copies[-1].start()

    for i, low in enumerate((0, layers - 8)):
        begin(direct_ref.at[:, pl.ds(low, 8), :], block_refs[2 * i])
        begin(sound_ref.at[pl.ds(low, 8), :], block_refs[2 * i + 1])
    for t, body_ref in zip(partners, body_refs):
        start = pl.multiple_of((here ^ t) * rows, rows)
        begin(direct_ref.at[:, pl.ds(start, rows), :], body_ref)
    for copy in copies[:4]:
        copy.wait()
    for i, (out_ref, row) in enumerate(((top_ref, 0), (bottom_ref, 7))):
        for part in range(2):
            for side in range(2):
                out_ref[2 * part + side, :] = block_refs[2 * i][part, row, side * mid : (side + 1) * mid]
        for side in range(2):
            out_ref[4 + side, :] = block_refs[2 * i + 1][row, side * mid : (side + 1) * mid]
            out_ref[6 + side, :] = jnp.zeros((mid,), jnp.float32)
    if lax.axis_size("slab") == 2:
        top_ref[...] = jnp.where(lax.axis_index("slab") == 0, bottom_ref[...], top_ref[...])
    for copy in copies[4:]:
        copy.wait()


def pack_kernel(half, rows, bare, field_ref, sound_ref, above_ref, below_ref, *out_refs):
    here = lax.axis_index("order") % half
    slab = lax.axis_index("slab")
    has_above, has_below = slab > 0, slab < lax.axis_size("slab") - 1
    width = field_ref.shape[2]
    mid = width // 2
    for t in range(half):
        site = here ^ t
        start = pl.multiple_of(site * rows, rows)
        block = 0
        for part in range(2):
            for low in range(0, rows, 8):
                for side in range(2):
                    out_refs[t][block * 8 : block * 8 + 8, :] = field_ref[
                        part, pl.ds(start + low, 8), side * mid : (side + 1) * mid
                    ]
                    block += 1
        before = jnp.maximum(start - 1, 0)
        after = jnp.minimum(start + rows, half * rows - 1)
        for part in range(2):
            for side in range(2):
                cut = slice(side * mid, (side + 1) * mid)
                from_slab = 2 * part + side
                edge = jnp.where(has_above, above_ref[from_slab : from_slab + 1, :], 0.0)
                up = jnp.where(site == 0, edge, field_ref[part, pl.ds(before, 1), cut])
                edge = jnp.where(has_below, below_ref[from_slab : from_slab + 1, :], 0.0)
                down = jnp.where(site == half - 1, edge, field_ref[part, pl.ds(after, 1), cut])
                for place, value in enumerate((up, down)):
                    at = part * 4 + place * 2 + side
                    out_refs[t][block * 8 + at : block * 8 + at + 1, :] = value
                    if t in bare:
                        out_refs[half + bare.index(t)][at : at + 1, :] = value
    site_ref = out_refs[half + len(bare)]
    start = pl.multiple_of(here * rows, rows)
    site_ref[0:rows, :] = sound_ref[pl.ds(start, rows), :]
    before = jnp.maximum(start - 1, 0)
    after = jnp.minimum(start + rows, half * rows - 1)
    for side in range(2):
        cut = slice(side * mid, (side + 1) * mid)
        edge = jnp.where(has_above, above_ref[4 + side : 5 + side, :], 0.0)
        site_ref[rows : rows + 1, cut] = jnp.where(here == 0, edge, sound_ref[pl.ds(before, 1), cut])
        edge = jnp.where(has_below, below_ref[4 + side : 5 + side, :], 0.0)
        site_ref[rows + 1 : rows + 2, cut] = jnp.where(here == half - 1, edge, sound_ref[pl.ds(after, 1), cut])


def table_kernel(orders, offsets_ref, temp_ref, gain_ref, turn_ref, coef_ref):
    step = 2.0 * math.pi / orders
    own = lax.axis_index("order")
    ids = lax.broadcasted_iota(jnp.int32, (orders, LANES), 0) ^ own
    angles = step * ids.astype(jnp.float32)
    turn_ref[0:orders, :] = jnp.cos(angles)
    turn_ref[orders:, :] = jnp.sin(angles)
    row = lax.broadcasted_iota(jnp.int32, (8, orders), 0)
    offset = jnp.zeros((8, orders), jnp.int32)
    for j in range(offsets_ref.shape[0]):
        offset = jnp.where(row == j, offsets_ref[j], offset)
    turns = (offset * lax.broadcasted_iota(jnp.int32, (8, orders), 1)) & (orders - 1)
    angles = step * turns.astype(jnp.float32)
    cos, sin = jnp.cos(angles), jnp.sin(angles)
    for p, (values_ref, wave, sign) in enumerate(
        ((temp_ref, cos, 1.0), (temp_ref, sin, -1.0), (gain_ref, cos, 1.0), (gain_ref, sin, -1.0))
    ):
        total = sign * jnp.sum(values_ref[...] * wave, axis=1, keepdims=True) / orders
        coef_ref[8 * p : 8 * p + 8, :] = jnp.broadcast_to(total, (8, LANES))


def split_kernel(full_ref, high_ref, low_ref):
    full = full_ref[...]
    high = full.astype(jnp.bfloat16)
    high_ref[...] = high
    low_ref[...] = (full - high.astype(jnp.float32)).astype(jnp.bfloat16)


def flame_kernel(half, rows, step, cells_ref, weight_ref, out_ref):
    width = out_ref.shape[1]
    shift = width.bit_length() - 1
    first = lax.axis_index("slab") * (half * rows) + lax.axis_index("order") % half * rows
    total = jnp.zeros((3 * rows, width), jnp.float32)
    for at in range(0, cells_ref.shape[0], step):
        cells = jnp.concatenate([cells_ref[i : i + 1, :] for i in range(at, at + step)], axis=1)
        weight = jnp.concatenate([weight_ref[i : i + 1, :] for i in range(at, at + step)], axis=1)
        cell_row = (cells >> shift) - first
        cell_col = cells & (width - 1)
        one = weight.astype(jnp.bfloat16).astype(jnp.float32)
        two = (weight - one).astype(jnp.bfloat16).astype(jnp.float32)
        three = weight - one - two
        hit = lax.broadcasted_iota(jnp.int32, (rows, step * LANES), 0) == cell_row
        left = jnp.concatenate([jnp.where(hit, x, 0.0) for x in (one, two, three)], axis=0)
        right = jnp.where(lax.broadcasted_iota(jnp.int32, (width, step * LANES), 0) == cell_col, 1.0, 0.0)
        total += lax.dot_general(
            left.astype(jnp.bfloat16),
            right.astype(jnp.bfloat16),
            (((1,), (1,)), ((), ())),
            preferred_element_type=jnp.float32,
        )
    out_ref[...] = total[:rows] + total[rows : 2 * rows] + total[2 * rows :]


def fill_flat(pieces, rows, flat_ref):
    mid = flat_ref.shape[1] // 2
    for i, (body_ref, _) in enumerate(pieces):
        first = i * 2 * rows
        if len(body_ref.shape) == 3:
            flat_ref[first : first + rows, :] = body_ref[0]
            flat_ref[first + rows : first + 2 * rows, :] = body_ref[1]
            continue
        block = 0
        for low in range(0, 2 * rows, 8):
            for side in range(2):
                flat_ref[first + low : first + low + 8, side * mid : (side + 1) * mid] = body_ref[
                    block * 8 : block * 8 + 8, :
                ]
                block += 1


def operate(pieces, rows, places, turn_ref, sound_ref, high_ref, low_ref, flat_ref, out_ref):
    width = sound_ref.shape[1]
    stacks = 2 * rows
    fill_flat(pieces, rows, flat_ref)
    flat = flat_ref[...]
    high = flat.astype(jnp.bfloat16)
    low_part = (flat - high.astype(jnp.float32)).astype(jnp.bfloat16)

    def dot(a, b):
        return jnp.dot(a, b, preferred_element_type=jnp.float32)

    across = dot(high, high_ref[...]) + (dot(high, low_ref[...]) + dot(low_part, high_ref[...]))
    orders = turn_ref.shape[0] // 2
    middle = sound_ref[0:rows, :]
    sound_up = jnp.concatenate([sound_ref[rows : rows + 1, :], middle[: rows - 1]], axis=0)
    sound_down = jnp.concatenate([middle[1:], sound_ref[rows + 1 : rows + 2, :]], axis=0)
    weight_up = 0.5 * (middle + sound_up)
    weight_down = 0.5 * (middle + sound_down)
    seam = 0.5 * (middle[:, width - 1 : width] + middle[:, 0:1])
    lane = lax.broadcasted_iota(jnp.int32, (rows, width), 1)
    for i, (_, halo_ref) in enumerate(pieces):
        at = places[i]
        cos_turn = turn_ref[at : at + 1, 0:1]
        sin_turn = turn_ref[orders + at : orders + at + 1, 0:1]
        fields = []
        for part in range(2):
            fields.append(flat[i * stacks + part * rows : i * stacks + (part + 1) * rows])
        firsts = [f[:, 0:1] for f in fields]
        lasts = [f[:, width - 1 : width] for f in fields]
        ahead = (
            cos_turn * firsts[0] - sin_turn * firsts[1],
            sin_turn * firsts[0] + cos_turn * firsts[1],
        )
        behind = (
            cos_turn * lasts[0] + sin_turn * lasts[1],
            cos_turn * lasts[1] - sin_turn * lasts[0],
        )
        halo_rows = halo_ref[halo_ref.shape[0] - 8 :, :]
        for part in range(2):
            field = fields[part]
            halo = halo_rows[part * 4 : part * 4 + 4]
            up = jnp.concatenate([halo[0:1], halo[1:2]], axis=1)
            down = jnp.concatenate([halo[2:3], halo[3:4]], axis=1)
            above = jnp.concatenate([up, field[: rows - 1]], axis=0)
            below = jnp.concatenate([field[1:], down], axis=0)
            result = weight_down * (field - below) + weight_up * (field - above)
            result = result + across[i * stacks + part * rows : i * stacks + (part + 1) * rows]
            last_add = seam * (lasts[part] - ahead[part])
            first_add = seam * (firsts[part] - behind[part])
            result = result + jnp.where(lane == width - 1, last_add, 0.0)
            result = result + jnp.where(lane == 0, first_add, 0.0)
            out_ref[i, part] = result
            out_ref[i, 2 + part] = field


def pair_up(refs, split):
    apart = [(refs[2 * i], refs[2 * i + 1]) for i in range(split)]
    return apart + [(r, r) for r in refs[2 * split :]]


def base_kernel(count, rows, places, split, turn_ref, *refs):
    taken = count + split
    pieces = pair_up(refs[:taken], split)
    sound_ref, high_ref, low_ref = refs[taken : taken + 3]
    out_ref, flat_ref = refs[-2:]
    operate(pieces, rows, places, turn_ref, sound_ref, high_ref, low_ref, flat_ref, out_ref)


def add_terms(coefs, source_ref, source, flame_ref, image_ref):
    temp_re, temp_im, gain_re, gain_im = coefs
    for at in range(0, flame_ref.shape[1], LANES):
        cut = slice(at, at + LANES)
        flame = flame_ref[:, cut]
        base_re = source_ref[source, 0, :, cut]
        base_im = source_ref[source, 1, :, cut]
        field_re = source_ref[source, 2, :, cut]
        field_im = source_ref[source, 3, :, cut]
        image_ref[0, :, cut] += (
            temp_re * base_re - temp_im * base_im + flame * (gain_re * field_re - gain_im * field_im)
        )
        image_ref[1, :, cut] += (
            temp_re * base_im + temp_im * base_re + flame * (gain_re * field_im + gain_im * field_re)
        )


def inner_products(rows, coefs, source_ref, source, adjoint_ref, flame_ref, sums_ref, at_re, at_im):
    temp_re, temp_im, gain_re, gain_im = coefs

    def fold(x):
        out = x[0:8]
        for low in range(8, rows, 8):
            out = out + x[low : low + 8]
        return out

    sums = [jnp.zeros((8, LANES), jnp.float32)] * 4
    for at in range(0, flame_ref.shape[1], LANES):
        cut = slice(at, at + LANES)
        flame = flame_ref[:, cut]
        adj_re = adjoint_ref[0, :, cut]
        adj_im = adjoint_ref[1, :, cut]
        base_re = source_ref[source, 0, :, cut]
        base_im = source_ref[source, 1, :, cut]
        field_re = flame * source_ref[source, 2, :, cut]
        field_im = flame * source_ref[source, 3, :, cut]
        sums[0] = sums[0] + fold(adj_re * base_re + adj_im * base_im)
        sums[1] = sums[1] + fold(adj_re * base_im - adj_im * base_re)
        sums[2] = sums[2] + fold(adj_re * field_re + adj_im * field_im)
        sums[3] = sums[3] + fold(adj_re * field_im - adj_im * field_re)
    sums_ref[at_re] = temp_re * sums[0] - temp_im * sums[1] + gain_re * sums[2] - gain_im * sums[3]
    sums_ref[at_im] = temp_re * sums[1] + temp_im * sums[0] + gain_re * sums[3] + gain_im * sums[2]


def coefs_of(coef_ref, j):
    return tuple(coef_ref[8 * p + j : 8 * p + j + 1, :] for p in range(4))


def source_of(half, offsets_ref, t, j):
    own = lax.axis_index("order")
    orders = 2 * half
    place = (((own ^ t) - offsets_ref[j] + orders) & (orders - 1)) ^ own
    quarter = half // 2
    later = half + (place & (quarter - 1)) * 2 + ((place & quarter) // quarter)
    return jnp.where(place < half, place, later)


def cross_order(half):
    return [t + far for t in range(half // 2) for far in (0, half // 2)]


def early_kernel(half, count_offs, ready, offsets_ref, coef_ref, own_ref, cross_ref, flame_ref, image_ref):
    for t in range(half):
        image_ref[t, 0] = own_ref[t, 0]
        image_ref[t, 1] = own_ref[t, 1]
        for j in range(count_offs):
            source = source_of(half, offsets_ref, t, j)

            @pl.when(source < half)
            def _(t=t, j=j, source=source):
                add_terms(coefs_of(coef_ref, j), own_ref, source, flame_ref, image_ref.at[t])

            @pl.when((source >= half) & (source < ready))
            def _(t=t, j=j, source=source):
                add_terms(coefs_of(coef_ref, j), cross_ref, source - half, flame_ref, image_ref.at[t])


def late_kernel(half, rows, slabs, count_offs, ready, offsets_ref, coef_ref, turn_ref, *refs):
    count = 2 * half - ready
    pieces = pair_up(refs[:count], 0)
    sound_ref, high_ref, low_ref, flame_ref, image_in_ref, sums_in_ref = refs[count : count + 6]
    adjoint_refs = refs[count + 6 : count + 6 + half]
    image_refs = refs[count + 6 + half : count + 6 + 2 * half]
    out_ref, site_ref, flat_ref, sums_ref = refs[count + 6 + 2 * half :]
    here = lax.axis_index("order") % half
    places = [half + t for t in cross_order(half)[-count:]]
    operate(pieces, rows, places, turn_ref, sound_ref, high_ref, low_ref, flat_ref, site_ref)
    sums_ref[...] = sums_in_ref[...]
    for t in range(half):
        image_refs[t][...] = image_in_ref[t]
        for j in range(count_offs):
            source = source_of(half, offsets_ref, t, j)

            @pl.when(source >= ready)
            def _(t=t, j=j, source=source):
                coefs = coefs_of(coef_ref, j)
                add_terms(coefs, site_ref, source - ready, flame_ref, image_refs[t])
                inner_products(
                    rows, coefs, site_ref, source - ready, adjoint_refs[t], flame_ref, sums_ref,
                    t * 2 * count_offs + j, t * 2 * count_offs + count_offs + j,
                )

    for t in range(half):
        totals = [
            jnp.sum(sums_ref[t * 2 * count_offs + i], axis=0, keepdims=True)
            for i in range(2 * count_offs)
        ]
        totals = jnp.concatenate(totals, axis=0)
        for slab in range(slabs):
            place = pl.multiple_of(((here ^ t) * slabs + slab) * 8, 8)
            out_ref[pl.ds(place, 8), :] = totals


def couple_kernel(half, rows, count_offs, ready, partners, offsets_ref, coef_ref, own_ref, cross_ref, *refs):
    adjoint_refs = refs[: len(partners)]
    flame_ref, *before_refs, sums_ref = refs[len(partners) :]
    for before_ref in before_refs:
        sums_ref[...] = before_ref[...]
    for adjoint_ref, t in zip(adjoint_refs, partners):
        for j in range(count_offs):
            source = source_of(half, offsets_ref, t, j)

            def product(source_ref, place, adjoint_ref=adjoint_ref, t=t, j=j):
                inner_products(
                    rows, coefs_of(coef_ref, j), source_ref, place, adjoint_ref, flame_ref, sums_ref,
                    t * 2 * count_offs + j, t * 2 * count_offs + count_offs + j,
                )

            @pl.when(source < half)
            def _(product=product, source=source):
                product(own_ref, source)

            @pl.when((source >= half) & (source < ready))
            def _(product=product, source=source):
                product(cross_ref, source - half)


def place_kernel(half, rows, count_offs, scale, *refs):
    piece_refs, parts_ref = refs[:half], refs[half]
    image_ref, out_ref, coupling_ref, sems = refs[half + 1 :]
    here = lax.axis_index("order") % half
    copies = []
    for t in range(half):
        start = pl.multiple_of((here ^ t) * rows, rows)
        copies.append(pltpu.make_async_copy(piece_refs[t], image_ref.at[:, pl.ds(start, rows), :], sems.at[t]))
        copies[-1].start()
    total = jnp.sum(jnp.sum(parts_ref[...], axis=0), axis=1, keepdims=True) * scale
    total = jnp.broadcast_to(total, (8, count_offs))
    row = lax.broadcasted_iota(jnp.int32, (8, count_offs), 0)
    col = lax.broadcasted_iota(jnp.int32, (8, count_offs), 1)
    for part in range(2):
        picked = jnp.where(row == part * count_offs + col, total, 0.0)
        coupling_ref[0, part : part + 1, :] = jnp.sum(picked, axis=0, keepdims=True)
    copies.append(pltpu.make_async_copy(coupling_ref, out_ref, sems.at[half]))
    copies[-1].start()
    for copy in copies:
        copy.wait()


VMEM_SPEC = pl.BlockSpec(memory_space=VMEM)


def call(kernel, ins, spaces, outs, scratch=(), out_specs=None, limit=LIMIT):
    return pl.pallas_call(
        kernel,
        out_shape=outs,
        in_specs=[pl.BlockSpec(memory_space=s) for s in spaces],
        out_specs=jax.tree.map(lambda _: VMEM_SPEC, outs) if out_specs is None else out_specs,
        scratch_shapes=list(scratch),
        compiler_params=pltpu.CompilerParams(vmem_limit_bytes=limit),
    )(*ins)


def local(
    direct, adjoint, sound, transverse, burner_temp, burner_gain, flame_cells, flame_weight, offsets
):
    f32 = jnp.float32
    orders = lax.axis_size("order")
    slabs = lax.axis_size("slab")
    order_now = lax.axis_index("order")
    half = orders // 2
    layers, width = direct.shape[2:]
    mid = width // 2
    rows = layers // half
    count_offs = offsets.shape[0]
    here = order_now % half
    block_rows = 2 * (rows // 8) * 2 * 8 + 8
    ready = orders - LATE

    def of(*shape, dtype=f32):
        return jax.ShapeDtypeStruct(shape, dtype)

    def swap(value, t):
        return lax.ppermute(value, "order", [(i, i ^ t) for i in range(orders)])

    field = direct[0]
    arrivals = cross_order(half)
    bare = arrivals[:BARE]
    *bodies, top, bottom = call(
        functools.partial(first_kernel, half, rows, bare),
        (field, sound),
        (pltpu.HBM, pltpu.HBM),
        [of(2, rows, width)] * BARE + [of(8, mid), of(8, mid)],
        [pltpu.VMEM((2, 8, width), f32), pltpu.VMEM((8, width), f32)] * 2
        + [pltpu.SemaphoreType.DMA((4 + BARE,))],
        limit=None,
    )
    if slabs == 2:
        above = below = lax.ppermute(top, "slab", [(0, 1), (1, 0)])
    else:
        above = lax.ppermute(bottom, "slab", [(i, i + 1) for i in range(slabs - 1)])
        below = lax.ppermute(top, "slab", [(i + 1, i) for i in range(slabs - 1)])

    sent = call(
        functools.partial(pack_kernel, half, rows, bare),
        (field, sound, above, below),
        (VMEM,) * 4,
        [of(block_rows, mid)] * half + [of(8, mid)] * BARE + [of(rows + 8, width)],
    )
    halos, sound_site = sent[half : half + BARE], sent[half + BARE]
    own = [sent[0]] + [swap(sent[t], t) for t in range(1, half)]
    pieces = []
    for t, body, halo in zip(bare, bodies, halos):
        pieces += [swap(body, half ^ t), swap(halo, half ^ t)]
    cross = [swap(sent[t], half ^ t) for t in arrivals[BARE:]]
    pieces += cross[: half - BARE - LATE]

    adjoint_cut = adjoint[0].reshape(2, half, rows, width)
    adj_sent = [lax.dynamic_index_in_dim(adjoint_cut, here ^ t, 1, keepdims=False) for t in range(half)]
    adj = [adj_sent[0]] + [swap(adj_sent[t], t) for t in range(1, half)]

    high, low = call(split_kernel, (transverse,), (VMEM,), [of(*transverse.shape, dtype=jnp.bfloat16)] * 2)
    turn, coef = call(
        functools.partial(table_kernel, orders),
        (offsets, burner_temp.reshape(1, -1), burner_gain.reshape(1, -1)),
        (SMEM, VMEM, VMEM),
        [of(2 * orders, LANES), of(32, LANES)],
    )
    flame = call(
        functools.partial(flame_kernel, half, rows, 4),
        (flame_cells.reshape(-1, LANES), flame_weight.reshape(-1, LANES)),
        (VMEM, VMEM),
        of(rows, width),
    )

    def base(pieces, places, split):
        return call(
            functools.partial(base_kernel, len(places), rows, places, split),
            (turn, *pieces, sound_site, high, low),
            (VMEM,) * (len(pieces) + 4),
            of(len(places), 4, rows, width),
            [pltpu.VMEM((len(places) * 2 * rows, width), f32)],
        )

    site_own = base(own, list(range(half)), 0)
    site_cross = base(pieces, [half + t for t in arrivals[:-LATE]], BARE)
    image_early = call(
        functools.partial(early_kernel, half, count_offs, ready),
        (offsets, coef, site_own, site_cross, flame),
        (SMEM,) + (VMEM,) * 4,
        of(half, 2, rows, width),
    )
    sums_shape = (half * 2 * count_offs, 8, LANES)
    sums_early = ()
    partners = [0] + far_first(half)
    for some in (partners[:-LAST], partners[-LAST:]):
        sums_early = call(
            functools.partial(couple_kernel, half, rows, count_offs, ready, some),
            (offsets, coef, site_own, site_cross, *(adj[t] for t in some), flame, *sums_early),
            (SMEM,) + (VMEM,) * (len(some) + 4 + len(sums_early)),
            [of(*sums_shape)],
        )
    *images, sums = call(
        functools.partial(late_kernel, half, rows, slabs, count_offs, ready),
        (offsets, coef, turn, *cross[half - BARE - LATE :], sound_site, high, low, flame, image_early, *sums_early, *adj),
        (SMEM,) + (VMEM,) * (LATE + half + 8),
        [of(2, rows, width)] * half + [of(half * slabs * 8, LANES)],
        [
            pltpu.VMEM((LATE, 4, rows, width), f32),
            pltpu.VMEM((LATE * 2 * rows, width), f32),
            pltpu.VMEM(sums_shape, f32),
        ],
    )

    back = [images[0]] + [swap(images[t], t) for t in range(1, half)]
    groups = [list(range(half * slabs)), list(range(half * slabs, orders * slabs))]
    parts = lax.all_to_all(
        sums.reshape(half * slabs, 8, LANES), ("order", "slab"), 0, 0, axis_index_groups=groups, tiled=True
    )
    scale = 1.0 / math.sqrt(layers * slabs * width)
    image, coupling = call(
        functools.partial(place_kernel, half, rows, count_offs, scale),
        (*back, parts),
        (VMEM,) * (half + 1),
        [of(2, layers, width), of(1, 2, count_offs)],
        [pltpu.VMEM((1, 2, count_offs), f32), pltpu.SemaphoreType.DMA((half + 1,))],
        [pl.BlockSpec(memory_space=pltpu.HBM)] * 2,
    )
    return (image[None], coupling)


def far_first(half):
    return sorted(range(1, half), key=lambda t: (-bin(t >> 1).count("1"), t & 1 if t > 1 else 2, -t))


def solution(mesh):
    in_specs = (
        P("order", None, "slab", None),
        P("order", None, "slab", None),
        P("slab", None),
        P(),
        P(),
        P(),
        P(),
        P(),
        P(),
    )
    out_specs = (P("order", None, "slab", None), P("order", None, None))

    return jax.shard_map(local, mesh=mesh, in_specs=in_specs, out_specs=out_specs, check_vma=False)
```

profile of v0, /device:TPU:0, one launch (start us, length us, event | category | flops | bytes accessed | tf_op | source)
XLA Modules:
  0.0 106.5 jit_solution(16737682906405844344)
XLA Ops:
  0.6 1.9 %shard_map.105 = (f32[2,16,1024]{2,1,0:T(8,128)}, f32[2,16,1024]{2,1,0:T(8,128)}, f32[8,512]{1,0:T(8,128)}, f32[8,512]{1,0:T(8,128)}) custom-call(f32[2,128,1024]{2,1,0:T(8,128)} %bitcast.40, f32[128,1024]{1,0:T(8,128)} %sound_ref.3), custom_call_target="tpu_custom_call" | custom-call | tf_op jit(solution)/shard_map/pallas_call | solution.py:400
  2.6 3.1 %collective-permute-start = (f32[8,512]{1,0:T(8,128)}, f32[8,512]{1,0:T(8,128)S(1)}, u32[]{:S(2)}, u32[]{:S(2)}) collective-permute-start(f32[8,512]{1,0:T(8,128)} %get-tuple-element.33), channel_id=1, source_target_pairs={{0,1},{1,0},{2,3},{3,2},{4,5},{5,4},{6,7},{7,6},{8,9},{9,8},{10,11... | collective-permute-start | bytes 49160 | tf_op jit(solution)/shard_map/ppermute | solution.py:445
  5.6 2.6 %collective-permute-start.10 = (f32[2,16,1024]{2,1,0:T(8,128)}, f32[2,16,1024]{2,1,0:T(8,128)S(1)}, u32[]{:S(2)}, u32[]{:S(2)}) collective-permute-start(f32[2,16,1024]{2,1,0:T(8,128)} %get-tuple-element.45), channel_id=1, source_target_pairs={{0,16},{2,18},{4,20},{6,22},{8,24},{10,26},{12,28},{14,30},{16,0},... | collective-permute-start | bytes 393224 | tf_op jit(solution)/shard_map/ppermute | solution.py:430
  10.7 1.8 %collective-permute-start.11 = (f32[8,512]{1,0:T(8,128)S(1)}, f32[8,512]{1,0:T(8,128)S(1)}, u32[]{:S(2)}, u32[]{:S(2)}) collective-permute-start(f32[8,512]{1,0:T(8,128)S(1)} %get-tuple-element.46), channel_id=1, source_target_pairs={{0,16},{2,18},{4,20},{6,22},{8,24},{10,26},{12,28},{14,30},{16,0},... | collective-permute-start | bytes 49160 | tf_op jit(solution)/shard_map/ppermute | solution.py:430
  13.6 7.8 %collective-permute-done.11.refs_1_ = f32[8,512]{1,0:T(8,128)S(1)} collective-permute-done((f32[8,512]{1,0:T(8,128)S(1)}, f32[8,512]{1,0:T(8,128)S(1)}, u32[]{:S(2)}, u32[]{:S(2)}) %collective-permute-start.11) | collective-permute-done | bytes 16416 | tf_op jit(solution)/shard_map/ppermute | solution.py:430
  24.9 1.8 %collective-permute-start.5 = (f32[72,512]{1,0:T(8,128)S(1)}, f32[72,512]{1,0:T(8,128)S(1)}, u32[]{:S(2)}, u32[]{:S(2)}) collective-permute-start(f32[72,512]{1,0:T(8,128)S(1)} %get-tuple-element.34), channel_id=1, source_target_pairs={{0,6},{2,4},{4,2},{6,0},{8,14},{10,12},{12,10},{14,8},{16,22},{18,... | collective-permute-start | bytes 442376 | tf_op jit(solution)/shard_map/ppermute | solution.py:430
  27.6 2.7 %collective-permute-done.22.refs_3_.refs_12_ = f32[2,16,1024]{2,1,0:T(8,128)S(1)} collective-permute-done((f32[2,16,1024]{2,1,0:T(8,128)S(1)}, f32[2,16,1024]{2,1,0:T(8,128)S(1)}, u32[]{:S(2)}, u32[]{:S(2)}) %collective-permute-start.22) | collective-permute-done | bytes 131104 | tf_op jit(solution)/shard_map/ppermute | solution.py:430
  31.8 1.9 %collective-permute-start.3 = (f32[72,512]{1,0:T(8,128)S(1)}, f32[72,512]{1,0:T(8,128)S(1)}, u32[]{:S(2)}, u32[]{:S(2)}) collective-permute-start(f32[72,512]{1,0:T(8,128)S(1)} %get-tuple-element.40), channel_id=1, source_target_pairs={{0,2},{2,0},{4,6},{6,4},{8,10},{10,8},{12,14},{14,12},{16,18},{18,... | collective-permute-start | bytes 442376 | tf_op jit(solution)/shard_map/ppermute | solution.py:430
  33.8 3.8 %collective-permute-start.16 = (f32[72,512]{1,0:T(8,128)S(1)}, f32[72,512]{1,0:T(8,128)S(1)}, u32[]{:S(2)}, u32[]{:S(2)}) collective-permute-start(f32[72,512]{1,0:T(8,128)S(1)} %get-tuple-element.41), channel_id=1, source_target_pairs={{0,20},{2,22},{4,16},{6,18},{8,28},{10,30},{12,24},{14,26},{16,4},... | collective-permute-start | bytes 442376 | tf_op jit(solution)/shard_map/ppermute | solution.py:430
  38.2 3.6 %collective-permute-start.15 = (f32[72,512]{1,0:T(8,128)S(1)}, f32[72,512]{1,0:T(8,128)S(1)}, u32[]{:S(2)}, u32[]{:S(2)}) collective-permute-start(f32[72,512]{1,0:T(8,128)S(1)} %get-tuple-element.43), channel_id=1, source_target_pairs={{0,26},{2,24},{4,30},{6,28},{8,18},{10,16},{12,22},{14,20},{16,10}... | collective-permute-start | bytes 442376 | tf_op jit(solution)/shard_map/ppermute | solution.py:430
  41.9 5.1 %collective-permute-start.7 = (f32[72,512]{1,0:T(8,128)S(1)}, f32[72,512]{1,0:T(8,128)S(1)}, u32[]{:S(2)}, u32[]{:S(2)}) collective-permute-start(f32[72,512]{1,0:T(8,128)S(1)} %get-tuple-element.43), channel_id=1, source_target_pairs={{0,10},{2,8},{4,14},{6,12},{8,2},{10,0},{12,6},{14,4},{16,26},{18,... | collective-permute-start | bytes 442376 | tf_op jit(solution)/shard_map/ppermute | solution.py:430
  46.9 4.4 %collective-permute-start.17 = (f32[72,512]{1,0:T(8,128)S(1)}, f32[72,512]{1,0:T(8,128)S(1)}, u32[]{:S(2)}, u32[]{:S(2)}) collective-permute-start(f32[72,512]{1,0:T(8,128)S(1)} %get-tuple-element.44), channel_id=1, source_target_pairs={{0,28},{2,30},{4,24},{6,26},{8,20},{10,22},{12,16},{14,18},{16,12}... | collective-permute-start | bytes 442376 | tf_op jit(solution)/shard_map/ppermute | solution.py:430
  52.7 3.9 %collective-permute-start.1 = (f32[72,512]{1,0:T(8,128)S(1)}, f32[72,512]{1,0:T(8,128)S(1)}, u32[]{:S(2)}, u32[]{:S(2)}) collective-permute-start(f32[72,512]{1,0:T(8,128)S(1)} %get-tuple-element.34), channel_id=1, source_target_pairs={{0,22},{2,20},{4,18},{6,16},{8,30},{10,28},{12,26},{14,24},{16,6},... | collective-permute-start | bytes 442376 | tf_op jit(solution)/shard_map/ppermute | solution.py:430
  58.2 2.1 %collective-permute-start.19 = (f32[2,16,1024]{2,1,0:T(8,128)S(1)}, f32[2,16,1024]{2,1,0:T(8,128)S(1)}, u32[]{:S(2)}, u32[]{:S(2)}) collective-permute-start(f32[2,16,1024]{2,1,0:T(8,128)S(1)} %get-tuple-element.66), channel_id=1, source_target_pairs={{0,2},{2,0},{4,6},{6,4},{8,10},{10,8},{12,14},{14,12},{16,18},{18,... | collective-permute-start | bytes 393224 | tf_op jit(solution)/shard_map/ppermute | solution.py:430
  61.4 2.2 %copy-done = f32[1024,1024]{1,0:T(8,128)S(1)} copy-done((f32[1024,1024]{1,0:T(8,128)S(1)}, f32[1024,1024]{1,0:T(8,128)}, u32[]{:S(2)}) %copy-start) | copy-done | bytes 4194328
  64.4 2.5 %shard_map.108.flame_ref.refs_6_.refs_2_.refs_5_ = f32[16,1024]{1,0:T(8,128)S(1)} custom-call(s32[32,128]{1,0:T(8,128)S(1)} %bitcast.43, f32[32,128]{1,0:T(8,128)S(1)} %bitcast.44), custom_call_target="tpu_custom_call" | custom-call | tf_op jit(solution)/shard_map/pallas_call | solution.py:400
  69.1 2.0 %shard_map.109.own_ref = f32[8,4,16,1024]{3,2,1,0:T(8,128)S(1)} custom-call(f32[32,128]{1,0:T(8,128)S(1)} %get-tuple-element.32.turn_ref, f32[72,512]{1,0:T(8,128)S(1)} %get-tuple-element.39.refs_0_, f32[72,512]{1,0:T(8,128)S(1)} %collective-permute-done.3.refs_1_, f32[72,512]{1,0:T(8,128)S(1)} %collective-permute-done.4.refs_2_, ...), custom_call_target="tpu_custom_call" | custom-call | tf_op jit(solution)/shard_map/pallas_call | solution.py:400
  71.1 2.7 %shard_map.111.refs_6_ = f32[8,2,16,1024]{3,2,1,0:T(8,128)S(1)} custom-call(s32[4]{0:T(128)S(1)} %copy-done.5, f32[32,128]{1,0:T(8,128)S(1)} %get-tuple-element.31.coef_ref, f32[8,4,16,1024]{3,2,1,0:T(8,128)S(1)} %shard_map.109.own_ref, f32[6,4,16,1024]{3,2,1,0:T(8,128)S(1)} %shard_map.110.cross_ref, f32[16,1024]{1,0:T(8,128)S(1)} %shard_map.108.flame_ref.refs_6_.refs_2_.refs_5_), custom_call_target="tpu_custom_call" | custom-call | tf_op jit(solution)/shard_map/pallas_call | solution.py:400
  73.8 2.2 %shard_map.112.refs_3_ = f32[64,8,128]{2,1,0:T(8,128)S(1)} custom-call(s32[4]{0:T(128)S(1)} %copy-done.5, f32[32,128]{1,0:T(8,128)S(1)} %get-tuple-element.31.coef_ref, f32[8,4,16,1024]{3,2,1,0:T(8,128)S(1)} %shard_map.109.own_ref, f32[6,4,16,1024]{3,2,1,0:T(8,128)S(1)} %shard_map.110.cross_ref, f32[2,16,1024]{2,1,0:T(8,128)S(1)} %get-tuple-element.65.refs_0_.refs_8_, ...), custom_call_target="tpu_custom_call" | custom-call | tf_op jit(solution)/shard_map/pallas_call | solution.py:400
  77.1 2.5 %shard_map.114 = (f32[2,16,1024]{2,1,0:T(8,128)S(1)}, f32[2,16,1024]{2,1,0:T(8,128)S(1)}, f32[2,16,1024]{2,1,0:T(8,128)S(1)}, f32[2,16,1024]{2,1,0:T(8,128)S(1)}...) custom-call(s32[4]{0:T(128)S(1)} %copy-done.5, ...), custom_call_target="tpu_custom_call" | custom-call | tf_op jit(solution)/shard_map/pallas_call | solution.py:400
  81.6 10.3 %collective-permute-start.28 = (f32[2,16,1024]{2,1,0:T(8,128)S(1)}, f32[2,16,1024]{2,1,0:T(8,128)S(1)}, u32[]{:S(2)}, u32[]{:S(2)}) collective-permute-start(f32[2,16,1024]{2,1,0:T(8,128)S(1)} %get-tuple-element.53), channel_id=1, source_target_pairs={{0,8},{2,10},{4,12},{6,14},{8,0},{10,2},{12,4},{14,6},{16,24},{18,... | collective-permute-start | bytes 393224 | tf_op jit(solution)/shard_map/ppermute | solution.py:430
  91.9 2.1 %collective-permute-start.30 = (f32[2,16,1024]{2,1,0:T(8,128)S(1)}, f32[2,16,1024]{2,1,0:T(8,128)S(1)}, u32[]{:S(2)}, u32[]{:S(2)}) collective-permute-start(f32[2,16,1024]{2,1,0:T(8,128)S(1)} %get-tuple-element.55), channel_id=1, source_target_pairs={{0,12},{2,14},{4,8},{6,10},{8,4},{10,6},{12,0},{14,2},{16,28},{18,... | collective-permute-start | bytes 393224 | tf_op jit(solution)/shard_map/ppermute | solution.py:430
  94.0 1.5 %collective-permute-start.31 = (f32[2,16,1024]{2,1,0:T(8,128)S(1)}, f32[2,16,1024]{2,1,0:T(8,128)S(1)}, u32[]{:S(2)}, u32[]{:S(2)}) collective-permute-start(f32[2,16,1024]{2,1,0:T(8,128)S(1)} %get-tuple-element.56), channel_id=1, source_target_pairs={{0,14},{2,12},{4,10},{6,8},{8,6},{10,4},{12,2},{14,0},{16,30},{18,... | collective-permute-start | bytes 393224 | tf_op jit(solution)/shard_map/ppermute | solution.py:430
  95.5 9.8 %all_to_all.5.refs_8_ = f32[16,8,128]{2,1,0:T(8,128)S(1)} all-to-all(f32[16,8,128]{2,1,0:T(8,128)S(1)} %bitcast.42), channel_id=1, replica_groups={{0,1,2,3,4,5,6,7,8,9,10,11,12,13,14,15},{16,17,18,19,20,21,22,23,24,25,..., dimensions={0} | all-to-all | bytes 131072 | tf_op jit(solution)/shard_map/all_to_all | solution.py:523
  (72 shorter events, 21.1 us)
Async XLA Ops:
  5.6 17.9 %collective-permute-start.10 = (f32[2,16,1024]{2,1,0:T(8,128)}, f32[2,16,1024]{2,1,0:T(8,128)S(1)}, u32[]{:S(2)}, u32[]{:S(2)}) collective-permute-start(f32[2,16,1024]{2,1,0:T(8,128)} %get-tuple-element.45), channel_id=1, source_target_pairs={{0,16},{2,18},{4,20},{6,22},{8,24},{10,26},{12,28},{14,30},{16,0},... | collective-permute-start | bytes 393224 | tf_op jit(solution)/shard_map/ppermute | solution.py:430
  8.2 16.7 %collective-permute-start.12 = (f32[2,16,1024]{2,1,0:T(8,128)}, f32[2,16,1024]{2,1,0:T(8,128)S(1)}, u32[]{:S(2)}, u32[]{:S(2)}) collective-permute-start(f32[2,16,1024]{2,1,0:T(8,128)} %get-tuple-element.47), channel_id=1, source_target_pairs={{0,24},{2,26},{4,28},{6,30},{8,16},{10,18},{12,20},{14,22},{16,8},... | collective-permute-start | bytes 393224 | tf_op jit(solution)/shard_map/ppermute | solution.py:430
  13.5 11.4 %collective-permute-start.24 = (f32[2,16,1024]{2,1,0:T(8,128)S(1)}, f32[2,16,1024]{2,1,0:T(8,128)S(1)}, u32[]{:S(2)}, u32[]{:S(2)}) collective-permute-start(f32[2,16,1024]{2,1,0:T(8,128)S(1)} %get-tuple-element.60), channel_id=1, source_target_pairs={{0,10},{2,8},{4,14},{6,12},{8,2},{10,0},{12,6},{14,4},{16,26},{18,... | collective-permute-start | bytes 393224 | tf_op jit(solution)/shard_map/ppermute | solution.py:430
  21.3 12.5 %collective-permute-start.6 = (f32[72,512]{1,0:T(8,128)S(1)}, f32[72,512]{1,0:T(8,128)S(1)}, u32[]{:S(2)}, u32[]{:S(2)}) collective-permute-start(f32[72,512]{1,0:T(8,128)S(1)} %get-tuple-element.42), channel_id=1, source_target_pairs={{0,8},{2,10},{4,12},{6,14},{8,0},{10,2},{12,4},{14,6},{16,24},{18,... | collective-permute-start | bytes 442376 | tf_op jit(solution)/shard_map/ppermute | solution.py:430
  24.9 12.7 %collective-permute-start.5 = (f32[72,512]{1,0:T(8,128)S(1)}, f32[72,512]{1,0:T(8,128)S(1)}, u32[]{:S(2)}, u32[]{:S(2)}) collective-permute-start(f32[72,512]{1,0:T(8,128)S(1)} %get-tuple-element.34), channel_id=1, source_target_pairs={{0,6},{2,4},{4,2},{6,0},{8,14},{10,12},{12,10},{14,8},{16,22},{18,... | collective-permute-start | bytes 442376 | tf_op jit(solution)/shard_map/ppermute | solution.py:430
  30.3 11.5 %collective-permute-start.14 = (f32[72,512]{1,0:T(8,128)S(1)}, f32[72,512]{1,0:T(8,128)S(1)}, u32[]{:S(2)}, u32[]{:S(2)}) collective-permute-start(f32[72,512]{1,0:T(8,128)S(1)} %get-tuple-element.40), channel_id=1, source_target_pairs={{0,18},{2,16},{4,22},{6,20},{8,26},{10,24},{12,30},{14,28},{16,2},... | collective-permute-start | bytes 442376 | tf_op jit(solution)/shard_map/ppermute | solution.py:430
  31.8 15.1 %collective-permute-start.3 = (f32[72,512]{1,0:T(8,128)S(1)}, f32[72,512]{1,0:T(8,128)S(1)}, u32[]{:S(2)}, u32[]{:S(2)}) collective-permute-start(f32[72,512]{1,0:T(8,128)S(1)} %get-tuple-element.40), channel_id=1, source_target_pairs={{0,2},{2,0},{4,6},{6,4},{8,10},{10,8},{12,14},{14,12},{16,18},{18,... | collective-permute-start | bytes 442376 | tf_op jit(solution)/shard_map/ppermute | solution.py:430
  33.8 18.9 %collective-permute-start.16 = (f32[72,512]{1,0:T(8,128)S(1)}, f32[72,512]{1,0:T(8,128)S(1)}, u32[]{:S(2)}, u32[]{:S(2)}) collective-permute-start(f32[72,512]{1,0:T(8,128)S(1)} %get-tuple-element.41), channel_id=1, source_target_pairs={{0,20},{2,22},{4,16},{6,18},{8,28},{10,30},{12,24},{14,26},{16,4},... | collective-permute-start | bytes 442376 | tf_op jit(solution)/shard_map/ppermute | solution.py:430
  37.6 15.1 %collective-permute-start.4 = (f32[72,512]{1,0:T(8,128)S(1)}, f32[72,512]{1,0:T(8,128)S(1)}, u32[]{:S(2)}, u32[]{:S(2)}) collective-permute-start(f32[72,512]{1,0:T(8,128)S(1)} %get-tuple-element.41), channel_id=1, source_target_pairs={{0,4},{2,6},{4,0},{6,2},{8,12},{10,14},{12,8},{14,10},{16,20},{18,... | collective-permute-start | bytes 442376 | tf_op jit(solution)/shard_map/ppermute | solution.py:430
  38.2 18.4 %collective-permute-start.15 = (f32[72,512]{1,0:T(8,128)S(1)}, f32[72,512]{1,0:T(8,128)S(1)}, u32[]{:S(2)}, u32[]{:S(2)}) collective-permute-start(f32[72,512]{1,0:T(8,128)S(1)} %get-tuple-element.43), channel_id=1, source_target_pairs={{0,26},{2,24},{4,30},{6,28},{8,18},{10,16},{12,22},{14,20},{16,10}... | collective-permute-start | bytes 442376 | tf_op jit(solution)/shard_map/ppermute | solution.py:430
  41.9 16.0 %collective-permute-start.7 = (f32[72,512]{1,0:T(8,128)S(1)}, f32[72,512]{1,0:T(8,128)S(1)}, u32[]{:S(2)}, u32[]{:S(2)}) collective-permute-start(f32[72,512]{1,0:T(8,128)S(1)} %get-tuple-element.43), channel_id=1, source_target_pairs={{0,10},{2,8},{4,14},{6,12},{8,2},{10,0},{12,6},{14,4},{16,26},{18,... | collective-permute-start | bytes 442376 | tf_op jit(solution)/shard_map/ppermute | solution.py:430
  46.9 11.3 %collective-permute-start.17 = (f32[72,512]{1,0:T(8,128)S(1)}, f32[72,512]{1,0:T(8,128)S(1)}, u32[]{:S(2)}, u32[]{:S(2)}) collective-permute-start(f32[72,512]{1,0:T(8,128)S(1)} %get-tuple-element.44), channel_id=1, source_target_pairs={{0,28},{2,30},{4,24},{6,26},{8,20},{10,22},{12,16},{14,18},{16,12}... | collective-permute-start | bytes 442376 | tf_op jit(solution)/shard_map/ppermute | solution.py:430
  52.7 24.4 %collective-permute-start.1 = (f32[72,512]{1,0:T(8,128)S(1)}, f32[72,512]{1,0:T(8,128)S(1)}, u32[]{:S(2)}, u32[]{:S(2)}) collective-permute-start(f32[72,512]{1,0:T(8,128)S(1)} %get-tuple-element.34), channel_id=1, source_target_pairs={{0,22},{2,20},{4,18},{6,16},{8,30},{10,28},{12,26},{14,24},{16,6},... | collective-permute-start | bytes 442376 | tf_op jit(solution)/shard_map/ppermute | solution.py:430
  56.6 20.5 %collective-permute-start.2 = (f32[72,512]{1,0:T(8,128)S(1)}, f32[72,512]{1,0:T(8,128)S(1)}, u32[]{:S(2)}, u32[]{:S(2)}) collective-permute-start(f32[72,512]{1,0:T(8,128)S(1)} %get-tuple-element.35), channel_id=1, source_target_pairs={{0,30},{2,28},{4,26},{6,24},{8,22},{10,20},{12,18},{14,16},{16,14}... | collective-permute-start | bytes 442376 | tf_op jit(solution)/shard_map/ppermute | solution.py:430
  57.8 16.0 %collective-permute-start.20 = (f32[2,16,1024]{2,1,0:T(8,128)S(1)}, f32[2,16,1024]{2,1,0:T(8,128)S(1)}, u32[]{:S(2)}, u32[]{:S(2)}) collective-permute-start(f32[2,16,1024]{2,1,0:T(8,128)S(1)} %get-tuple-element.64), channel_id=1, source_target_pairs={{0,12},{2,14},{4,8},{6,10},{8,4},{10,6},{12,0},{14,2},{16,28},{18,... | collective-permute-start | bytes 393224 | tf_op jit(solution)/shard_map/ppermute | solution.py:430
  58.2 17.8 %collective-permute-start.19 = (f32[2,16,1024]{2,1,0:T(8,128)S(1)}, f32[2,16,1024]{2,1,0:T(8,128)S(1)}, u32[]{:S(2)}, u32[]{:S(2)}) collective-permute-start(f32[2,16,1024]{2,1,0:T(8,128)S(1)} %get-tuple-element.66), channel_id=1, source_target_pairs={{0,2},{2,0},{4,6},{6,4},{8,10},{10,8},{12,14},{14,12},{16,18},{18,... | collective-permute-start | bytes 393224 | tf_op jit(solution)/shard_map/ppermute | solution.py:430
  60.3 15.7 %collective-permute-start.18 = (f32[2,16,1024]{2,1,0:T(8,128)S(1)}, f32[2,16,1024]{2,1,0:T(8,128)S(1)}, u32[]{:S(2)}, u32[]{:S(2)}) collective-permute-start(f32[2,16,1024]{2,1,0:T(8,128)S(1)} %get-tuple-element.67), channel_id=1, source_target_pairs={{0,6},{2,4},{4,2},{6,0},{8,14},{10,12},{12,10},{14,8},{16,22},{18,... | collective-permute-start | bytes 393224 | tf_op jit(solution)/shard_map/ppermute | solution.py:430
  79.6 12.2 %collective-permute-start.25 = (f32[2,16,1024]{2,1,0:T(8,128)S(1)}, f32[2,16,1024]{2,1,0:T(8,128)S(1)}, u32[]{:S(2)}, u32[]{:S(2)}) collective-permute-start(f32[2,16,1024]{2,1,0:T(8,128)S(1)} %get-tuple-element.50), channel_id=1, source_target_pairs={{0,2},{2,0},{4,6},{6,4},{8,10},{10,8},{12,14},{14,12},{16,18},{18,... | collective-permute-start | bytes 393224 | tf_op jit(solution)/shard_map/ppermute | solution.py:430
  80.2 13.8 %collective-permute-start.26 = (f32[2,16,1024]{2,1,0:T(8,128)S(1)}, f32[2,16,1024]{2,1,0:T(8,128)S(1)}, u32[]{:S(2)}, u32[]{:S(2)}) collective-permute-start(f32[2,16,1024]{2,1,0:T(8,128)S(1)} %get-tuple-element.51), channel_id=1, source_target_pairs={{0,4},{2,6},{4,0},{6,2},{8,12},{10,14},{12,8},{14,10},{16,20},{18,... | collective-permute-start | bytes 393224 | tf_op jit(solution)/shard_map/ppermute | solution.py:430
  80.8 24.5 %collective-permute-start.27 = (f32[2,16,1024]{2,1,0:T(8,128)S(1)}, f32[2,16,1024]{2,1,0:T(8,128)S(1)}, u32[]{:S(2)}, u32[]{:S(2)}) collective-permute-start(f32[2,16,1024]{2,1,0:T(8,128)S(1)} %get-tuple-element.52), channel_id=1, source_target_pairs={{0,6},{2,4},{4,2},{6,0},{8,14},{10,12},{12,10},{14,8},{16,22},{18,... | collective-permute-start | bytes 393224 | tf_op jit(solution)/shard_map/ppermute | solution.py:430
  81.6 23.7 %collective-permute-start.28 = (f32[2,16,1024]{2,1,0:T(8,128)S(1)}, f32[2,16,1024]{2,1,0:T(8,128)S(1)}, u32[]{:S(2)}, u32[]{:S(2)}) collective-permute-start(f32[2,16,1024]{2,1,0:T(8,128)S(1)} %get-tuple-element.53), channel_id=1, source_target_pairs={{0,8},{2,10},{4,12},{6,14},{8,0},{10,2},{12,4},{14,6},{16,24},{18,... | collective-permute-start | bytes 393224 | tf_op jit(solution)/shard_map/ppermute | solution.py:430
  91.9 13.4 %collective-permute-start.29 = (f32[2,16,1024]{2,1,0:T(8,128)S(1)}, f32[2,16,1024]{2,1,0:T(8,128)S(1)}, u32[]{:S(2)}, u32[]{:S(2)}) collective-permute-start(f32[2,16,1024]{2,1,0:T(8,128)S(1)} %get-tuple-element.54), channel_id=1, source_target_pairs={{0,10},{2,8},{4,14},{6,12},{8,2},{10,0},{12,6},{14,4},{16,26},{18,... | collective-permute-start | bytes 393224 | tf_op jit(solution)/shard_map/ppermute | solution.py:430
  91.9 13.4 %collective-permute-start.30 = (f32[2,16,1024]{2,1,0:T(8,128)S(1)}, f32[2,16,1024]{2,1,0:T(8,128)S(1)}, u32[]{:S(2)}, u32[]{:S(2)}) collective-permute-start(f32[2,16,1024]{2,1,0:T(8,128)S(1)} %get-tuple-element.55), channel_id=1, source_target_pairs={{0,12},{2,14},{4,8},{6,10},{8,4},{10,6},{12,0},{14,2},{16,28},{18,... | collective-permute-start | bytes 393224 | tf_op jit(solution)/shard_map/ppermute | solution.py:430
  94.0 11.3 %collective-permute-start.31 = (f32[2,16,1024]{2,1,0:T(8,128)S(1)}, f32[2,16,1024]{2,1,0:T(8,128)S(1)}, u32[]{:S(2)}, u32[]{:S(2)}) collective-permute-start(f32[2,16,1024]{2,1,0:T(8,128)S(1)} %get-tuple-element.56), channel_id=1, source_target_pairs={{0,14},{2,12},{4,10},{6,8},{8,6},{10,4},{12,2},{14,0},{16,30},{18,... | collective-permute-start | bytes 393224 | tf_op jit(solution)/shard_map/ppermute | solution.py:430
  (17 other events, 91.2 us)
where the time goes:
time: 107 us
  starting transfers between devices  60.6 us (57%)
  Pallas kernels  18.9 us (18%)
  waiting for transfers between devices  12.8 us (12%)
  blocking collectives  9.81 us (9%)
  local copies, waits for them, and re-layouts  3.36 us (3%)
    ppermute x31, starting transfers between devices, swap(): return lax.ppermute(value, 'order', [(i, i ^ t) for i in range(orders)])  57.6 us
    pallas_call x12, Pallas kernels, call(): pl.pallas_call(kernel, out_shape=outs, in_specs=[pl.BlockSpec(memory_spac...  18.9 us
    ppermute x31, waiting for transfers between devices, swap(): return lax.ppermute(value, 'order', [(i, i ^ t) for i in range(orders)])  12.8 us
    all_to_all x1, blocking collectives, local(): lax.all_to_all(sums.reshape(half * slabs, 8, LANES), ('order', 'slab'), 0...  9.81 us
    unnamed x18, local copies, waits for them, and re-layouts  3.28 us
    ppermute x1, starting transfers between devices, local(): above = below = lax.ppermute(top, 'slab', [(0, 1), (1, 0)])  3.06 us
  transfers between devices with their start and end apart: 32, of which 5 were waited for; matrix products, arithmetic and copies ran while one was open for 0% of the time, Pallas kernels for 13%

commit v1 on v0

--- a/solution.py
+++ b/solution.py
@@ -177,7 +177,8 @@
     def dot(a, b):
         return jnp.dot(a, b, preferred_element_type=jnp.float32)
 
-    across = dot(high, high_ref[...]) + (dot(high, low_ref[...]) + dot(low_part, high_ref[...]))
+    both = dot(jnp.concatenate([high, low_part], axis=0), high_ref[...])
+    across = both[: flat.shape[0]] + (dot(high, low_ref[...]) + both[flat.shape[0] :])
     orders = turn_ref.shape[0] // 2
     middle = sound_ref[0:rows, :]
     sound_up = jnp.concatenate([sound_ref[rows : rows + 1, :], middle[: rows - 1]], axis=0)
@@ -498,7 +499,7 @@
     )
     sums_shape = (half * 2 * count_offs, 8, LANES)
     sums_early = ()
-    partners = [0] + far_first(half)
+    partners = [0] + sorted(even_first(half), key=lambda t: t & 1 and t >= half // 2)
     for some in (partners[:-LAST], partners[-LAST:]):
         sums_early = call(
             functools.partial(couple_kernel, half, rows, count_offs, ready, some),
@@ -535,8 +536,8 @@
     return (image[None], coupling)
 
 
-def far_first(half):
-    return sorted(range(1, half), key=lambda t: (-bin(t >> 1).count("1"), t & 1 if t > 1 else 2, -t))
+def even_first(half):
+    return sorted(range(1, half), key=lambda t: (t & 1, -t))
 
 
 def solution(mesh):

time: 107 us -> 106 us (level)
  starting transfers between devices: 60.6 us -> 58.7 us
  waiting for transfers between devices: 12.8 us -> 14.6 us
    ppermute x31, starting transfers between devices: 57.6 us -> 55.6 us  [swap(): return lax.ppermute(value, 'order', [(i, i ^ t) for i in range(orders)])]
    ppermute x31, waiting for transfers between devices: 12.8 us -> 14.6 us  [swap(): return lax.ppermute(value, 'order', [(i, i ^ t) for i in range(orders)])]
  transfers between devices with their start and end apart: 32 -> 32, of which waited for: 5 -> 6; matrix products, arithmetic and copies ran while one was open for 0% -> 0% of each run, Pallas kernels for 13% -> 13%
where the time goes in v1:
time: 106 us
  starting transfers between devices  58.7 us (55%)
  Pallas kernels  18.7 us (18%)
  waiting for transfers between devices  14.6 us (14%)
  blocking collectives  9.8 us (9%)
  local copies, waits for them, and re-layouts  3.36 us (3%)
    ppermute x31, starting transfers between devices, swap(): return lax.ppermute(value, 'order', [(i, i ^ t) for i in range(orders)])  55.6 us
    pallas_call x12, Pallas kernels, call(): pl.pallas_call(kernel, out_shape=outs, in_specs=[pl.BlockSpec(memory_spac...  18.7 us
    ppermute x31, waiting for transfers between devices, swap(): return lax.ppermute(value, 'order', [(i, i ^ t) for i in range(orders)])  14.6 us
    all_to_all x1, blocking collectives, local(): lax.all_to_all(sums.reshape(half * slabs, 8, LANES), ('order', 'slab'), 0...  9.8 us
    unnamed x18, local copies, waits for them, and re-layouts  3.28 us
    ppermute x1, starting transfers between devices, local(): above = below = lax.ppermute(top, 'slab', [(0, 1), (1, 0)])  3.06 us
  transfers between devices with their start and end apart: 32, of which 6 were waited for; matrix products, arithmetic and copies ran while one was open for 0% of the time, Pallas kernels for 13%

profile of v1, /device:TPU:0, one launch (start us, length us, event | category | flops | bytes accessed | tf_op | source)
XLA Modules:
  0.0 106.1 jit_solution(18258300142928142039)
XLA Ops:
  0.6 1.9 %shard_map.105 = (f32[2,16,1024]{2,1,0:T(8,128)}, f32[2,16,1024]{2,1,0:T(8,128)}, f32[8,512]{1,0:T(8,128)}, f32[8,512]{1,0:T(8,128)}) custom-call(f32[2,128,1024]{2,1,0:T(8,128)} %bitcast.40, f32[128,1024]{1,0:T(8,128)} %sound_ref.3), custom_call_target="tpu_custom_call" | custom-call | tf_op jit(solution)/shard_map/pallas_call | solution.py:401
  2.6 3.1 %collective-permute-start = (f32[8,512]{1,0:T(8,128)}, f32[8,512]{1,0:T(8,128)S(1)}, u32[]{:S(2)}, u32[]{:S(2)}) collective-permute-start(f32[8,512]{1,0:T(8,128)} %get-tuple-element.33), channel_id=1, source_target_pairs={{0,1},{1,0},{2,3},{3,2},{4,5},{5,4},{6,7},{7,6},{8,9},{9,8},{10,11... | collective-permute-start | bytes 49160 | tf_op jit(solution)/shard_map/ppermute | solution.py:446
  5.6 2.6 %collective-permute-start.10 = (f32[2,16,1024]{2,1,0:T(8,128)}, f32[2,16,1024]{2,1,0:T(8,128)S(1)}, u32[]{:S(2)}, u32[]{:S(2)}) collective-permute-start(f32[2,16,1024]{2,1,0:T(8,128)} %get-tuple-element.45), channel_id=1, source_target_pairs={{0,16},{2,18},{4,20},{6,22},{8,24},{10,26},{12,28},{14,30},{16,0},... | collective-permute-start | bytes 393224 | tf_op jit(solution)/shard_map/ppermute | solution.py:431
  10.7 1.8 %collective-permute-start.11 = (f32[8,512]{1,0:T(8,128)S(1)}, f32[8,512]{1,0:T(8,128)S(1)}, u32[]{:S(2)}, u32[]{:S(2)}) collective-permute-start(f32[8,512]{1,0:T(8,128)S(1)} %get-tuple-element.46), channel_id=1, source_target_pairs={{0,16},{2,18},{4,20},{6,22},{8,24},{10,26},{12,28},{14,30},{16,0},... | collective-permute-start | bytes 49160 | tf_op jit(solution)/shard_map/ppermute | solution.py:431
  13.6 7.8 %collective-permute-done.11.refs_1_ = f32[8,512]{1,0:T(8,128)S(1)} collective-permute-done((f32[8,512]{1,0:T(8,128)S(1)}, f32[8,512]{1,0:T(8,128)S(1)}, u32[]{:S(2)}, u32[]{:S(2)}) %collective-permute-start.11) | collective-permute-done | bytes 16416 | tf_op jit(solution)/shard_map/ppermute | solution.py:431
  28.0 2.6 %collective-permute-done.22.refs_3_.refs_10_ = f32[2,16,1024]{2,1,0:T(8,128)S(1)} collective-permute-done((f32[2,16,1024]{2,1,0:T(8,128)S(1)}, f32[2,16,1024]{2,1,0:T(8,128)S(1)}, u32[]{:S(2)}, u32[]{:S(2)}) %collective-permute-start.22) | collective-permute-done | bytes 131104 | tf_op jit(solution)/shard_map/ppermute | solution.py:431
  30.6 3.0 %collective-permute-start.14 = (f32[72,512]{1,0:T(8,128)S(1)}, f32[72,512]{1,0:T(8,128)S(1)}, u32[]{:S(2)}, u32[]{:S(2)}) collective-permute-start(f32[72,512]{1,0:T(8,128)S(1)} %get-tuple-element.40), channel_id=1, source_target_pairs={{0,18},{2,16},{4,22},{6,20},{8,26},{10,24},{12,30},{14,28},{16,2},... | collective-permute-start | bytes 442376 | tf_op jit(solution)/shard_map/ppermute | solution.py:431
  34.7 2.1 %collective-permute-done.5.refs_3_ = f32[72,512]{1,0:T(8,128)S(1)} collective-permute-done((f32[72,512]{1,0:T(8,128)S(1)}, f32[72,512]{1,0:T(8,128)S(1)}, u32[]{:S(2)}, u32[]{:S(2)}) %collective-permute-start.5) | collective-permute-done | bytes 147488 | tf_op jit(solution)/shard_map/ppermute | solution.py:431
  38.2 2.4 %collective-permute-start.15 = (f32[72,512]{1,0:T(8,128)S(1)}, f32[72,512]{1,0:T(8,128)S(1)}, u32[]{:S(2)}, u32[]{:S(2)}) collective-permute-start(f32[72,512]{1,0:T(8,128)S(1)} %get-tuple-element.43), channel_id=1, source_target_pairs={{0,26},{2,24},{4,30},{6,28},{8,18},{10,16},{12,22},{14,20},{16,10}... | collective-permute-start | bytes 442376 | tf_op jit(solution)/shard_map/ppermute | solution.py:431
  40.6 5.8 %collective-permute-start.7 = (f32[72,512]{1,0:T(8,128)S(1)}, f32[72,512]{1,0:T(8,128)S(1)}, u32[]{:S(2)}, u32[]{:S(2)}) collective-permute-start(f32[72,512]{1,0:T(8,128)S(1)} %get-tuple-element.43), channel_id=1, source_target_pairs={{0,10},{2,8},{4,14},{6,12},{8,2},{10,0},{12,6},{14,4},{16,26},{18,... | collective-permute-start | bytes 442376 | tf_op jit(solution)/shard_map/ppermute | solution.py:431
  46.5 5.3 %collective-permute-start.17 = (f32[72,512]{1,0:T(8,128)S(1)}, f32[72,512]{1,0:T(8,128)S(1)}, u32[]{:S(2)}, u32[]{:S(2)}) collective-permute-start(f32[72,512]{1,0:T(8,128)S(1)} %get-tuple-element.44), channel_id=1, source_target_pairs={{0,28},{2,30},{4,24},{6,26},{8,20},{10,22},{12,16},{14,18},{16,12}... | collective-permute-start | bytes 442376 | tf_op jit(solution)/shard_map/ppermute | solution.py:431
  52.1 3.4 %collective-permute-start.1 = (f32[72,512]{1,0:T(8,128)S(1)}, f32[72,512]{1,0:T(8,128)S(1)}, u32[]{:S(2)}, u32[]{:S(2)}) collective-permute-start(f32[72,512]{1,0:T(8,128)S(1)} %get-tuple-element.34), channel_id=1, source_target_pairs={{0,22},{2,20},{4,18},{6,16},{8,30},{10,28},{12,26},{14,24},{16,6},... | collective-permute-start | bytes 442376 | tf_op jit(solution)/shard_map/ppermute | solution.py:431
  56.9 3.4 %collective-permute-start.20 = (f32[2,16,1024]{2,1,0:T(8,128)S(1)}, f32[2,16,1024]{2,1,0:T(8,128)S(1)}, u32[]{:S(2)}, u32[]{:S(2)}) collective-permute-start(f32[2,16,1024]{2,1,0:T(8,128)S(1)} %get-tuple-element.64), channel_id=1, source_target_pairs={{0,12},{2,14},{4,8},{6,10},{8,4},{10,6},{12,0},{14,2},{16,28},{18,... | collective-permute-start | bytes 393224 | tf_op jit(solution)/shard_map/ppermute | solution.py:431
  60.3 6.2 %collective-permute-start.19 = (f32[2,16,1024]{2,1,0:T(8,128)S(1)}, f32[2,16,1024]{2,1,0:T(8,128)S(1)}, u32[]{:S(2)}, u32[]{:S(2)}) collective-permute-start(f32[2,16,1024]{2,1,0:T(8,128)S(1)} %get-tuple-element.66), channel_id=1, source_target_pairs={{0,10},{2,8},{4,14},{6,12},{8,2},{10,0},{12,6},{14,4},{16,26},{18,... | collective-permute-start | bytes 393224 | tf_op jit(solution)/shard_map/ppermute | solution.py:431
  66.5 2.5 %collective-permute-start.18 = (f32[2,16,1024]{2,1,0:T(8,128)S(1)}, f32[2,16,1024]{2,1,0:T(8,128)S(1)}, u32[]{:S(2)}, u32[]{:S(2)}) collective-permute-start(f32[2,16,1024]{2,1,0:T(8,128)S(1)} %get-tuple-element.67), channel_id=1, source_target_pairs={{0,14},{2,12},{4,10},{6,8},{8,6},{10,4},{12,2},{14,0},{16,30},{18,... | collective-permute-start | bytes 393224 | tf_op jit(solution)/shard_map/ppermute | solution.py:431
  69.0 2.2 %copy-done = f32[1024,1024]{1,0:T(8,128)S(1)} copy-done((f32[1024,1024]{1,0:T(8,128)S(1)}, f32[1024,1024]{1,0:T(8,128)}, u32[]{:S(2)}) %copy-start) | copy-done | bytes 4194328
  72.0 2.5 %shard_map.108.flame_ref.refs_6_.refs_2_.refs_5_ = f32[16,1024]{1,0:T(8,128)S(1)} custom-call(s32[32,128]{1,0:T(8,128)S(1)} %bitcast.43, f32[32,128]{1,0:T(8,128)S(1)} %bitcast.44), custom_call_target="tpu_custom_call" | custom-call | tf_op jit(solution)/shard_map/pallas_call | solution.py:401
  76.8 2.0 %shard_map.109.own_ref = f32[8,4,16,1024]{3,2,1,0:T(8,128)S(1)} custom-call(f32[32,128]{1,0:T(8,128)S(1)} %get-tuple-element.32.turn_ref, f32[72,512]{1,0:T(8,128)S(1)} %get-tuple-element.39.refs_0_, f32[72,512]{1,0:T(8,128)S(1)} %collective-permute-done.3.refs_1_, f32[72,512]{1,0:T(8,128)S(1)} %collective-permute-done.4.refs_2_, ...), custom_call_target="tpu_custom_call" | custom-call | tf_op jit(solution)/shard_map/pallas_call | solution.py:401
  78.8 2.7 %shard_map.111.refs_6_ = f32[8,2,16,1024]{3,2,1,0:T(8,128)S(1)} custom-call(s32[4]{0:T(128)S(1)} %copy-done.5, f32[32,128]{1,0:T(8,128)S(1)} %get-tuple-element.31.coef_ref, f32[8,4,16,1024]{3,2,1,0:T(8,128)S(1)} %shard_map.109.own_ref, f32[6,4,16,1024]{3,2,1,0:T(8,128)S(1)} %shard_map.110.cross_ref, f32[16,1024]{1,0:T(8,128)S(1)} %shard_map.108.flame_ref.refs_6_.refs_2_.refs_5_), custom_call_target="tpu_custom_call" | custom-call | tf_op jit(solution)/shard_map/pallas_call | solution.py:401
  81.6 2.2 %shard_map.112.refs_3_ = f32[64,8,128]{2,1,0:T(8,128)S(1)} custom-call(s32[4]{0:T(128)S(1)} %copy-done.5, f32[32,128]{1,0:T(8,128)S(1)} %get-tuple-element.31.coef_ref, f32[8,4,16,1024]{3,2,1,0:T(8,128)S(1)} %shard_map.109.own_ref, f32[6,4,16,1024]{3,2,1,0:T(8,128)S(1)} %shard_map.110.cross_ref, f32[2,16,1024]{2,1,0:T(8,128)S(1)} %get-tuple-element.65.refs_0_.refs_8_, ...), custom_call_target="tpu_custom_call" | custom-call | tf_op jit(solution)/shard_map/pallas_call | solution.py:401
  84.9 2.1 %shard_map.114 = (f32[2,16,1024]{2,1,0:T(8,128)S(1)}, f32[2,16,1024]{2,1,0:T(8,128)S(1)}, f32[2,16,1024]{2,1,0:T(8,128)S(1)}, f32[2,16,1024]{2,1,0:T(8,128)S(1)}...) custom-call(s32[4]{0:T(128)S(1)} %copy-done.5, ...), custom_call_target="tpu_custom_call" | custom-call | tf_op jit(solution)/shard_map/pallas_call | solution.py:401
  88.9 1.7 %collective-permute-start.28 = (f32[2,16,1024]{2,1,0:T(8,128)S(1)}, f32[2,16,1024]{2,1,0:T(8,128)S(1)}, u32[]{:S(2)}, u32[]{:S(2)}) collective-permute-start(f32[2,16,1024]{2,1,0:T(8,128)S(1)} %get-tuple-element.53), channel_id=1, source_target_pairs={{0,8},{2,10},{4,12},{6,14},{8,0},{10,2},{12,4},{14,6},{16,24},{18,... | collective-permute-start | bytes 393224 | tf_op jit(solution)/shard_map/ppermute | solution.py:431
  91.0 2.5 %collective-permute-start.30 = (f32[2,16,1024]{2,1,0:T(8,128)S(1)}, f32[2,16,1024]{2,1,0:T(8,128)S(1)}, u32[]{:S(2)}, u32[]{:S(2)}) collective-permute-start(f32[2,16,1024]{2,1,0:T(8,128)S(1)} %get-tuple-element.55), channel_id=1, source_target_pairs={{0,12},{2,14},{4,8},{6,10},{8,4},{10,6},{12,0},{14,2},{16,28},{18,... | collective-permute-start | bytes 393224 | tf_op jit(solution)/shard_map/ppermute | solution.py:431
  95.0 9.8 %all_to_all.5.refs_8_ = f32[16,8,128]{2,1,0:T(8,128)S(1)} all-to-all(f32[16,8,128]{2,1,0:T(8,128)S(1)} %bitcast.42), channel_id=1, replica_groups={{0,1,2,3,4,5,6,7,8,9,10,11,12,13,14,15},{16,17,18,19,20,21,22,23,24,25,..., dimensions={0} | all-to-all | bytes 131072 | tf_op jit(solution)/shard_map/all_to_all | solution.py:524
  (72 shorter events, 23.4 us)
Async XLA Ops:
  5.6 17.1 %collective-permute-start.10 = (f32[2,16,1024]{2,1,0:T(8,128)}, f32[2,16,1024]{2,1,0:T(8,128)S(1)}, u32[]{:S(2)}, u32[]{:S(2)}) collective-permute-start(f32[2,16,1024]{2,1,0:T(8,128)} %get-tuple-element.45), channel_id=1, source_target_pairs={{0,16},{2,18},{4,20},{6,22},{8,24},{10,26},{12,28},{14,30},{16,0},... | collective-permute-start | bytes 393224 | tf_op jit(solution)/shard_map/ppermute | solution.py:431
  8.2 15.3 %collective-permute-start.12 = (f32[2,16,1024]{2,1,0:T(8,128)}, f32[2,16,1024]{2,1,0:T(8,128)S(1)}, u32[]{:S(2)}, u32[]{:S(2)}) collective-permute-start(f32[2,16,1024]{2,1,0:T(8,128)} %get-tuple-element.47), channel_id=1, source_target_pairs={{0,24},{2,26},{4,28},{6,30},{8,16},{10,18},{12,20},{14,22},{16,8},... | collective-permute-start | bytes 393224 | tf_op jit(solution)/shard_map/ppermute | solution.py:431
  10.7 10.6 %collective-permute-start.11 = (f32[8,512]{1,0:T(8,128)S(1)}, f32[8,512]{1,0:T(8,128)S(1)}, u32[]{:S(2)}, u32[]{:S(2)}) collective-permute-start(f32[8,512]{1,0:T(8,128)S(1)} %get-tuple-element.46), channel_id=1, source_target_pairs={{0,16},{2,18},{4,20},{6,22},{8,24},{10,26},{12,28},{14,30},{16,0},... | collective-permute-start | bytes 49160 | tf_op jit(solution)/shard_map/ppermute | solution.py:431
  13.5 11.5 %collective-permute-start.24 = (f32[2,16,1024]{2,1,0:T(8,128)S(1)}, f32[2,16,1024]{2,1,0:T(8,128)S(1)}, u32[]{:S(2)}, u32[]{:S(2)}) collective-permute-start(f32[2,16,1024]{2,1,0:T(8,128)S(1)} %get-tuple-element.60), channel_id=1, source_target_pairs={{0,2},{2,0},{4,6},{6,4},{8,10},{10,8},{12,14},{14,12},{16,18},{18,... | collective-permute-start | bytes 393224 | tf_op jit(solution)/shard_map/ppermute | solution.py:431
  21.3 12.7 %collective-permute-start.6 = (f32[72,512]{1,0:T(8,128)S(1)}, f32[72,512]{1,0:T(8,128)S(1)}, u32[]{:S(2)}, u32[]{:S(2)}) collective-permute-start(f32[72,512]{1,0:T(8,128)S(1)} %get-tuple-element.42), channel_id=1, source_target_pairs={{0,8},{2,10},{4,12},{6,14},{8,0},{10,2},{12,4},{14,6},{16,24},{18,... | collective-permute-start | bytes 442376 | tf_op jit(solution)/shard_map/ppermute | solution.py:431
  24.9 11.9 %collective-permute-start.5 = (f32[72,512]{1,0:T(8,128)S(1)}, f32[72,512]{1,0:T(8,128)S(1)}, u32[]{:S(2)}, u32[]{:S(2)}) collective-permute-start(f32[72,512]{1,0:T(8,128)S(1)} %get-tuple-element.34), channel_id=1, source_target_pairs={{0,6},{2,4},{4,2},{6,0},{8,14},{10,12},{12,10},{14,8},{16,22},{18,... | collective-permute-start | bytes 442376 | tf_op jit(solution)/shard_map/ppermute | solution.py:431
  27.7 10.5 %collective-permute-start.9 = (f32[72,512]{1,0:T(8,128)S(1)}, f32[72,512]{1,0:T(8,128)S(1)}, u32[]{:S(2)}, u32[]{:S(2)}) collective-permute-start(f32[72,512]{1,0:T(8,128)S(1)} %get-tuple-element.35), channel_id=1, source_target_pairs={{0,14},{2,12},{4,10},{6,8},{8,6},{10,4},{12,2},{14,0},{16,30},{18,... | collective-permute-start | bytes 442376 | tf_op jit(solution)/shard_map/ppermute | solution.py:431
  33.6 12.9 %collective-permute-start.3 = (f32[72,512]{1,0:T(8,128)S(1)}, f32[72,512]{1,0:T(8,128)S(1)}, u32[]{:S(2)}, u32[]{:S(2)}) collective-permute-start(f32[72,512]{1,0:T(8,128)S(1)} %get-tuple-element.40), channel_id=1, source_target_pairs={{0,2},{2,0},{4,6},{6,4},{8,10},{10,8},{12,14},{14,12},{16,18},{18,... | collective-permute-start | bytes 442376 | tf_op jit(solution)/shard_map/ppermute | solution.py:431
  34.1 17.7 %collective-permute-start.16 = (f32[72,512]{1,0:T(8,128)S(1)}, f32[72,512]{1,0:T(8,128)S(1)}, u32[]{:S(2)}, u32[]{:S(2)}) collective-permute-start(f32[72,512]{1,0:T(8,128)S(1)} %get-tuple-element.41), channel_id=1, source_target_pairs={{0,20},{2,22},{4,16},{6,18},{8,28},{10,30},{12,24},{14,26},{16,4},... | collective-permute-start | bytes 442376 | tf_op jit(solution)/shard_map/ppermute | solution.py:431
  36.8 15.3 %collective-permute-start.4 = (f32[72,512]{1,0:T(8,128)S(1)}, f32[72,512]{1,0:T(8,128)S(1)}, u32[]{:S(2)}, u32[]{:S(2)}) collective-permute-start(f32[72,512]{1,0:T(8,128)S(1)} %get-tuple-element.41), channel_id=1, source_target_pairs={{0,4},{2,6},{4,0},{6,2},{8,12},{10,14},{12,8},{14,10},{16,20},{18,... | collective-permute-start | bytes 442376 | tf_op jit(solution)/shard_map/ppermute | solution.py:431
  38.2 17.3 %collective-permute-start.15 = (f32[72,512]{1,0:T(8,128)S(1)}, f32[72,512]{1,0:T(8,128)S(1)}, u32[]{:S(2)}, u32[]{:S(2)}) collective-permute-start(f32[72,512]{1,0:T(8,128)S(1)} %get-tuple-element.43), channel_id=1, source_target_pairs={{0,26},{2,24},{4,30},{6,28},{8,18},{10,16},{12,22},{14,20},{16,10}... | collective-permute-start | bytes 442376 | tf_op jit(solution)/shard_map/ppermute | solution.py:431
  40.6 16.3 %collective-permute-start.7 = (f32[72,512]{1,0:T(8,128)S(1)}, f32[72,512]{1,0:T(8,128)S(1)}, u32[]{:S(2)}, u32[]{:S(2)}) collective-permute-start(f32[72,512]{1,0:T(8,128)S(1)} %get-tuple-element.43), channel_id=1, source_target_pairs={{0,10},{2,8},{4,14},{6,12},{8,2},{10,0},{12,6},{14,4},{16,26},{18,... | collective-permute-start | bytes 442376 | tf_op jit(solution)/shard_map/ppermute | solution.py:431
  46.5 13.8 %collective-permute-start.17 = (f32[72,512]{1,0:T(8,128)S(1)}, f32[72,512]{1,0:T(8,128)S(1)}, u32[]{:S(2)}, u32[]{:S(2)}) collective-permute-start(f32[72,512]{1,0:T(8,128)S(1)} %get-tuple-element.44), channel_id=1, source_target_pairs={{0,28},{2,30},{4,24},{6,26},{8,20},{10,22},{12,16},{14,18},{16,12}... | collective-permute-start | bytes 442376 | tf_op jit(solution)/shard_map/ppermute | solution.py:431
  51.8 14.7 %collective-permute-start.8 = (f32[72,512]{1,0:T(8,128)S(1)}, f32[72,512]{1,0:T(8,128)S(1)}, u32[]{:S(2)}, u32[]{:S(2)}) collective-permute-start(f32[72,512]{1,0:T(8,128)S(1)} %get-tuple-element.44), channel_id=1, source_target_pairs={{0,12},{2,14},{4,8},{6,10},{8,4},{10,6},{12,0},{14,2},{16,28},{18,... | collective-permute-start | bytes 442376 | tf_op jit(solution)/shard_map/ppermute | solution.py:431
  52.1 32.7 %collective-permute-start.1 = (f32[72,512]{1,0:T(8,128)S(1)}, f32[72,512]{1,0:T(8,128)S(1)}, u32[]{:S(2)}, u32[]{:S(2)}) collective-permute-start(f32[72,512]{1,0:T(8,128)S(1)} %get-tuple-element.34), channel_id=1, source_target_pairs={{0,22},{2,20},{4,18},{6,16},{8,30},{10,28},{12,26},{14,24},{16,6},... | collective-permute-start | bytes 442376 | tf_op jit(solution)/shard_map/ppermute | solution.py:431
  55.5 29.4 %collective-permute-start.2 = (f32[72,512]{1,0:T(8,128)S(1)}, f32[72,512]{1,0:T(8,128)S(1)}, u32[]{:S(2)}, u32[]{:S(2)}) collective-permute-start(f32[72,512]{1,0:T(8,128)S(1)} %get-tuple-element.35), channel_id=1, source_target_pairs={{0,30},{2,28},{4,26},{6,24},{8,22},{10,20},{12,18},{14,16},{16,14}... | collective-permute-start | bytes 442376 | tf_op jit(solution)/shard_map/ppermute | solution.py:431
  56.9 24.7 %collective-permute-start.20 = (f32[2,16,1024]{2,1,0:T(8,128)S(1)}, f32[2,16,1024]{2,1,0:T(8,128)S(1)}, u32[]{:S(2)}, u32[]{:S(2)}) collective-permute-start(f32[2,16,1024]{2,1,0:T(8,128)S(1)} %get-tuple-element.64), channel_id=1, source_target_pairs={{0,12},{2,14},{4,8},{6,10},{8,4},{10,6},{12,0},{14,2},{16,28},{18,... | collective-permute-start | bytes 393224 | tf_op jit(solution)/shard_map/ppermute | solution.py:431
  60.3 23.5 %collective-permute-start.19 = (f32[2,16,1024]{2,1,0:T(8,128)S(1)}, f32[2,16,1024]{2,1,0:T(8,128)S(1)}, u32[]{:S(2)}, u32[]{:S(2)}) collective-permute-start(f32[2,16,1024]{2,1,0:T(8,128)S(1)} %get-tuple-element.66), channel_id=1, source_target_pairs={{0,10},{2,8},{4,14},{6,12},{8,2},{10,0},{12,6},{14,4},{16,26},{18,... | collective-permute-start | bytes 393224 | tf_op jit(solution)/shard_map/ppermute | solution.py:431
  66.5 17.3 %collective-permute-start.18 = (f32[2,16,1024]{2,1,0:T(8,128)S(1)}, f32[2,16,1024]{2,1,0:T(8,128)S(1)}, u32[]{:S(2)}, u32[]{:S(2)}) collective-permute-start(f32[2,16,1024]{2,1,0:T(8,128)S(1)} %get-tuple-element.67), channel_id=1, source_target_pairs={{0,14},{2,12},{4,10},{6,8},{8,6},{10,4},{12,2},{14,0},{16,30},{18,... | collective-permute-start | bytes 393224 | tf_op jit(solution)/shard_map/ppermute | solution.py:431
  88.9 16.0 %collective-permute-start.27 = (f32[2,16,1024]{2,1,0:T(8,128)S(1)}, f32[2,16,1024]{2,1,0:T(8,128)S(1)}, u32[]{:S(2)}, u32[]{:S(2)}) collective-permute-start(f32[2,16,1024]{2,1,0:T(8,128)S(1)} %get-tuple-element.52), channel_id=1, source_target_pairs={{0,6},{2,4},{4,2},{6,0},{8,14},{10,12},{12,10},{14,8},{16,22},{18,... | collective-permute-start | bytes 393224 | tf_op jit(solution)/shard_map/ppermute | solution.py:431
  88.9 15.9 %collective-permute-start.28 = (f32[2,16,1024]{2,1,0:T(8,128)S(1)}, f32[2,16,1024]{2,1,0:T(8,128)S(1)}, u32[]{:S(2)}, u32[]{:S(2)}) collective-permute-start(f32[2,16,1024]{2,1,0:T(8,128)S(1)} %get-tuple-element.53), channel_id=1, source_target_pairs={{0,8},{2,10},{4,12},{6,14},{8,0},{10,2},{12,4},{14,6},{16,24},{18,... | collective-permute-start | bytes 393224 | tf_op jit(solution)/shard_map/ppermute | solution.py:431
  90.6 14.2 %collective-permute-start.29 = (f32[2,16,1024]{2,1,0:T(8,128)S(1)}, f32[2,16,1024]{2,1,0:T(8,128)S(1)}, u32[]{:S(2)}, u32[]{:S(2)}) collective-permute-start(f32[2,16,1024]{2,1,0:T(8,128)S(1)} %get-tuple-element.54), channel_id=1, source_target_pairs={{0,10},{2,8},{4,14},{6,12},{8,2},{10,0},{12,6},{14,4},{16,26},{18,... | collective-permute-start | bytes 393224 | tf_op jit(solution)/shard_map/ppermute | solution.py:431
  91.0 13.9 %collective-permute-start.30 = (f32[2,16,1024]{2,1,0:T(8,128)S(1)}, f32[2,16,1024]{2,1,0:T(8,128)S(1)}, u32[]{:S(2)}, u32[]{:S(2)}) collective-permute-start(f32[2,16,1024]{2,1,0:T(8,128)S(1)} %get-tuple-element.55), channel_id=1, source_target_pairs={{0,12},{2,14},{4,8},{6,10},{8,4},{10,6},{12,0},{14,2},{16,28},{18,... | collective-permute-start | bytes 393224 | tf_op jit(solution)/shard_map/ppermute | solution.py:431
  93.8 11.1 %collective-permute-start.31 = (f32[2,16,1024]{2,1,0:T(8,128)S(1)}, f32[2,16,1024]{2,1,0:T(8,128)S(1)}, u32[]{:S(2)}, u32[]{:S(2)}) collective-permute-start(f32[2,16,1024]{2,1,0:T(8,128)S(1)} %get-tuple-element.56), channel_id=1, source_target_pairs={{0,14},{2,12},{4,10},{6,8},{8,6},{10,4},{12,2},{14,0},{16,30},{18,... | collective-permute-start | bytes 393224 | tf_op jit(solution)/shard_map/ppermute | solution.py:431
  (17 other events, 86.9 us)

commit v2 on v1

--- a/solution.py
+++ b/solution.py
@@ -13,7 +13,7 @@
 SMEM = pltpu.SMEM
 LANES = 128
 LATE = 2
-BARE = 2
+BARE = 1
 LAST = 2
 LIMIT = 20 * 1024 * 1024
 
@@ -51,7 +51,7 @@
         copy.wait()
 
 
-def pack_kernel(half, rows, bare, field_ref, sound_ref, above_ref, below_ref, *out_refs):
+def pack_kernel(half, rows, bare, field_ref, above_ref, below_ref, *out_refs):
     here = lax.axis_index("order") % half
     slab = lax.axis_index("slab")
     has_above, has_below = slab > 0, slab < lax.axis_size("slab") - 1
@@ -83,7 +83,13 @@
                     out_refs[t][block * 8 + at : block * 8 + at + 1, :] = value
                     if t in bare:
                         out_refs[half + bare.index(t)][at : at + 1, :] = value
-    site_ref = out_refs[half + len(bare)]
+
+
+def sound_kernel(half, rows, sound_ref, above_ref, below_ref, site_ref):
+    here = lax.axis_index("order") % half
+    slab = lax.axis_index("slab")
+    has_above, has_below = slab > 0, slab < lax.axis_size("slab") - 1
+    mid = sound_ref.shape[1] // 2
     start = pl.multiple_of(here * rows, rows)
     site_ref[0:rows, :] = sound_ref[pl.ds(start, rows), :]
     before = jnp.maximum(start - 1, 0)
@@ -450,11 +456,14 @@
 
     sent = call(
         functools.partial(pack_kernel, half, rows, bare),
-        (field, sound, above, below),
-        (VMEM,) * 4,
-        [of(block_rows, mid)] * half + [of(8, mid)] * BARE + [of(rows + 8, width)],
-    )
-    halos, sound_site = sent[half : half + BARE], sent[half + BARE]
+        (field, above, below),
+        (VMEM,) * 3,
+        [of(block_rows, mid)] * half + [of(8, mid)] * BARE,
+    )
+    halos = sent[half:]
+    sound_site = call(
+        functools.partial(sound_kernel, half, rows), (sound, above, below), (VMEM,) * 3, of(rows + 8, width)
+    )
     own = [sent[0]] + [swap(sent[t], t) for t in range(1, half)]
     pieces = []
     for t, body, halo in zip(bare, bodies, halos):

time: 106 us -> 109 us (1.028)
  waiting for transfers between devices: 14.6 us -> 16.9 us
    ppermute x1, waiting for transfers between devices: 0.01 us -> 2.22 us  [local(): above = below = lax.ppermute(top, 'slab', [(0, 1), (1, 0)])]
    ppermute x1, starting transfers between devices: 3.06 us -> 1.58 us  [local(): above = below = lax.ppermute(top, 'slab', [(0, 1), (1, 0)])]
    squeeze x1, local copies, waits for them, and re-layouts: 0.08 us -> 1.37 us  [local(): lax.dynamic_index_in_dim(adjoint_cut, here ^ t, 1, keepdims=False)]
    ppermute x31 -> x30, starting transfers between devices: 55.6 us -> 56.3 us  [swap(): return lax.ppermute(value, 'order', [(i, i ^ t) for i in range(orders)])]
    ppermute x31 -> x30, waiting for transfers between devices: 14.6 us -> 14.7 us  [swap(): return lax.ppermute(value, 'order', [(i, i ^ t) for i in range(orders)])]
    pallas_call x12 -> x13, Pallas kernels: 18.7 us -> 18.6 us  [call(): pl.pallas_call(kernel, out_shape=outs, in_specs=[pl.BlockSpec(memory_spac...]
  transfers between devices with their start and end apart: 32 -> 31, of which waited for: 6 -> 7; matrix products, arithmetic and copies ran while one was open for 0% -> 1% of each run, Pallas kernels for 13% -> 13%
where the time goes in v2:
time: 109 us
  starting transfers between devices  57.9 us (53%)
  Pallas kernels  18.6 us (17%)
  waiting for transfers between devices  16.9 us (16%)
  blocking collectives  10.8 us (10%)
  local copies, waits for them, and re-layouts  3.61 us (3%)
    ppermute x30, starting transfers between devices, swap(): return lax.ppermute(value, 'order', [(i, i ^ t) for i in range(orders)])  56.3 us
    pallas_call x13, Pallas kernels, call(): pl.pallas_call(kernel, out_shape=outs, in_specs=[pl.BlockSpec(memory_spac...  18.6 us
    ppermute x30, waiting for transfers between devices, swap(): return lax.ppermute(value, 'order', [(i, i ^ t) for i in range(orders)])  14.7 us
    all_to_all x1, blocking collectives, local(): lax.all_to_all(sums.reshape(half * slabs, 8, LANES), ('order', 'slab'), 0...  10.8 us
    unnamed x18, local copies, waits for them, and re-layouts  2.25 us
    ppermute x1, waiting for transfers between devices, local(): above = below = lax.ppermute(top, 'slab', [(0, 1), (1, 0)])  2.22 us
  transfers between devices with their start and end apart: 31, of which 7 were waited for; matrix products, arithmetic and copies ran while one was open for 1% of the time, Pallas kernels for 13%

profile of v2, /device:TPU:0, one launch (start us, length us, event | category | flops | bytes accessed | tf_op | source)
XLA Modules:
  0.0 108.9 jit_solution(15444432834857796929)
XLA Ops:
  0.6 1.8 %shard_map.105 = (f32[2,16,1024]{2,1,0:T(8,128)}, f32[8,512]{1,0:T(8,128)}, f32[8,512]{1,0:T(8,128)}) custom-call(f32[2,128,1024]{2,1,0:T(8,128)} %bitcast.40, f32[128,1024]{1,0:T(8,128)} %sound_ref.3), custom_call_target="tpu_custom_call" | custom-call | tf_op jit(solution)/shard_map/pallas_call | solution.py:407
  2.5 4.1 %collective-permute-start.10 = (f32[2,16,1024]{2,1,0:T(8,128)}, f32[2,16,1024]{2,1,0:T(8,128)S(1)}, u32[]{:S(2)}, u32[]{:S(2)}) collective-permute-start(f32[2,16,1024]{2,1,0:T(8,128)} %get-tuple-element.41), channel_id=1, source_target_pairs={{0,16},{2,18},{4,20},{6,22},{8,24},{10,26},{12,28},{14,30},{16,0},... | collective-permute-start | bytes 393224 | tf_op jit(solution)/shard_map/ppermute | solution.py:437
  9.6 2.2 %collective-permute-done.above_ref.below_ref = f32[8,512]{1,0:T(8,128)S(1)} collective-permute-done((f32[8,512]{1,0:T(8,128)S(1)}, f32[8,512]{1,0:T(8,128)S(1)}, u32[]{:S(2)}, u32[]{:S(2)}) %collective-permute-start) | collective-permute-done | bytes 16416 | tf_op jit(solution)/shard_map/ppermute | solution.py:452
  12.8 2.4 %collective-permute-start.9 = (f32[72,512]{1,0:T(8,128)S(1)}, f32[72,512]{1,0:T(8,128)S(1)}, u32[]{:S(2)}, u32[]{:S(2)}) collective-permute-start(f32[72,512]{1,0:T(8,128)S(1)} %get-tuple-element.32), channel_id=1, source_target_pairs={{0,14},{2,12},{4,10},{6,8},{8,6},{10,4},{12,2},{14,0},{16,30},{18,... | collective-permute-start | bytes 442376 | tf_op jit(solution)/shard_map/ppermute | solution.py:437
  18.3 1.6 %collective-permute-start.20 = (f32[2,16,1024]{2,1,0:T(8,128)S(1)}, f32[2,16,1024]{2,1,0:T(8,128)S(1)}, u32[]{:S(2)}, u32[]{:S(2)}) collective-permute-start(f32[2,16,1024]{2,1,0:T(8,128)S(1)} %get-tuple-element.57), channel_id=1, source_target_pairs={{0,8},{2,10},{4,12},{6,14},{8,0},{10,2},{12,4},{14,6},{16,24},{18,... | collective-permute-start | bytes 393224 | tf_op jit(solution)/shard_map/ppermute | solution.py:437
  19.9 4.0 %collective-permute-done.22.refs_4_.refs_11_ = f32[2,16,1024]{2,1,0:T(8,128)S(1)} collective-permute-done((f32[2,16,1024]{2,1,0:T(8,128)S(1)}, f32[2,16,1024]{2,1,0:T(8,128)S(1)}, u32[]{:S(2)}, u32[]{:S(2)}) %collective-permute-start.22) | collective-permute-done | bytes 131104 | tf_op jit(solution)/shard_map/ppermute | solution.py:437
  24.0 2.8 %collective-permute-start.13 = (f32[72,512]{1,0:T(8,128)S(1)}, f32[72,512]{1,0:T(8,128)S(1)}, u32[]{:S(2)}, u32[]{:S(2)}) collective-permute-start(f32[72,512]{1,0:T(8,128)S(1)} %get-tuple-element.36), channel_id=1, source_target_pairs={{0,18},{2,16},{4,22},{6,20},{8,26},{10,24},{12,30},{14,28},{16,2},... | collective-permute-start | bytes 442376 | tf_op jit(solution)/shard_map/ppermute | solution.py:437
  27.2 2.7 %collective-permute-start.15 = (f32[72,512]{1,0:T(8,128)S(1)}, f32[72,512]{1,0:T(8,128)S(1)}, u32[]{:S(2)}, u32[]{:S(2)}) collective-permute-start(f32[72,512]{1,0:T(8,128)S(1)} %get-tuple-element.37), channel_id=1, source_target_pairs={{0,20},{2,22},{4,16},{6,18},{8,28},{10,30},{12,24},{14,26},{16,4},... | collective-permute-start | bytes 442376 | tf_op jit(solution)/shard_map/ppermute | solution.py:437
  32.8 7.3 %collective-permute-done.13.refs_3_ = f32[72,512]{1,0:T(8,128)S(1)} collective-permute-done((f32[72,512]{1,0:T(8,128)S(1)}, f32[72,512]{1,0:T(8,128)S(1)}, u32[]{:S(2)}, u32[]{:S(2)}) %collective-permute-start.13) | collective-permute-done | bytes 147488 | tf_op jit(solution)/shard_map/ppermute | solution.py:437
  41.7 2.5 %collective-permute-start.14 = (f32[72,512]{1,0:T(8,128)S(1)}, f32[72,512]{1,0:T(8,128)S(1)}, u32[]{:S(2)}, u32[]{:S(2)}) collective-permute-start(f32[72,512]{1,0:T(8,128)S(1)} %get-tuple-element.39), channel_id=1, source_target_pairs={{0,26},{2,24},{4,30},{6,28},{8,18},{10,16},{12,22},{14,20},{16,10}... | collective-permute-start | bytes 442376 | tf_op jit(solution)/shard_map/ppermute | solution.py:437
  45.4 3.2 %collective-permute-start.16 = (f32[72,512]{1,0:T(8,128)S(1)}, f32[72,512]{1,0:T(8,128)S(1)}, u32[]{:S(2)}, u32[]{:S(2)}) collective-permute-start(f32[72,512]{1,0:T(8,128)S(1)} %get-tuple-element.40), channel_id=1, source_target_pairs={{0,28},{2,30},{4,24},{6,26},{8,20},{10,22},{12,16},{14,18},{16,12}... | collective-permute-start | bytes 442376 | tf_op jit(solution)/shard_map/ppermute | solution.py:437
  48.6 3.2 %collective-permute-start.8 = (f32[72,512]{1,0:T(8,128)S(1)}, f32[72,512]{1,0:T(8,128)S(1)}, u32[]{:S(2)}, u32[]{:S(2)}) collective-permute-start(f32[72,512]{1,0:T(8,128)S(1)} %get-tuple-element.40), channel_id=1, source_target_pairs={{0,12},{2,14},{4,8},{6,10},{8,4},{10,6},{12,0},{14,2},{16,28},{18,... | collective-permute-start | bytes 442376 | tf_op jit(solution)/shard_map/ppermute | solution.py:437
  52.5 2.4 %collective-permute-start.2 = (f32[72,512]{1,0:T(8,128)S(1)}, f32[72,512]{1,0:T(8,128)S(1)}, u32[]{:S(2)}, u32[]{:S(2)}) collective-permute-start(f32[72,512]{1,0:T(8,128)S(1)} %get-tuple-element.32), channel_id=1, source_target_pairs={{0,30},{2,28},{4,26},{6,24},{8,22},{10,20},{12,18},{14,16},{16,14}... | collective-permute-start | bytes 442376 | tf_op jit(solution)/shard_map/ppermute | solution.py:437
  54.9 5.7 %collective-permute-start.19 = (f32[2,16,1024]{2,1,0:T(8,128)S(1)}, f32[2,16,1024]{2,1,0:T(8,128)S(1)}, u32[]{:S(2)}, u32[]{:S(2)}) collective-permute-start(f32[2,16,1024]{2,1,0:T(8,128)S(1)} %get-tuple-element.58), channel_id=1, source_target_pairs={{0,12},{2,14},{4,8},{6,10},{8,4},{10,6},{12,0},{14,2},{16,28},{18,... | collective-permute-start | bytes 393224 | tf_op jit(solution)/shard_map/ppermute | solution.py:437
  60.6 9.1 %collective-permute-start.18 = (f32[2,16,1024]{2,1,0:T(8,128)S(1)}, f32[2,16,1024]{2,1,0:T(8,128)S(1)}, u32[]{:S(2)}, u32[]{:S(2)}) collective-permute-start(f32[2,16,1024]{2,1,0:T(8,128)S(1)} %get-tuple-element.60), channel_id=1, source_target_pairs={{0,10},{2,8},{4,14},{6,12},{8,2},{10,0},{12,6},{14,4},{16,26},{18,... | collective-permute-start | bytes 393224 | tf_op jit(solution)/shard_map/ppermute | solution.py:437
  69.7 2.2 %copy-done = f32[1024,1024]{1,0:T(8,128)S(1)} copy-done((f32[1024,1024]{1,0:T(8,128)S(1)}, f32[1024,1024]{1,0:T(8,128)}, u32[]{:S(2)}) %copy-start) | copy-done | bytes 4194328
  72.7 2.5 %shard_map.109.flame_ref.refs_6_.refs_2_.refs_5_ = f32[16,1024]{1,0:T(8,128)S(1)} custom-call(s32[32,128]{1,0:T(8,128)S(1)} %bitcast.43, f32[32,128]{1,0:T(8,128)S(1)} %bitcast.44), custom_call_target="tpu_custom_call" | custom-call | tf_op jit(solution)/shard_map/pallas_call | solution.py:407
  77.5 2.0 %shard_map.110.own_ref = f32[8,4,16,1024]{3,2,1,0:T(8,128)S(1)} custom-call(f32[32,128]{1,0:T(8,128)S(1)} %get-tuple-element.29.turn_ref, f32[72,512]{1,0:T(8,128)S(1)} %get-tuple-element.35.refs_0_, f32[72,512]{1,0:T(8,128)S(1)} %collective-permute-done.3.refs_1_, f32[72,512]{1,0:T(8,128)S(1)} %collective-permute-done.4.refs_2_, ...), custom_call_target="tpu_custom_call" | custom-call | tf_op jit(solution)/shard_map/pallas_call | solution.py:407
  79.6 2.7 %shard_map.112.refs_6_ = f32[8,2,16,1024]{3,2,1,0:T(8,128)S(1)} custom-call(s32[4]{0:T(128)S(1)} %copy-done.5, f32[32,128]{1,0:T(8,128)S(1)} %get-tuple-element.28.coef_ref, f32[8,4,16,1024]{3,2,1,0:T(8,128)S(1)} %shard_map.110.own_ref, f32[6,4,16,1024]{3,2,1,0:T(8,128)S(1)} %shard_map.111.cross_ref, f32[16,1024]{1,0:T(8,128)S(1)} %shard_map.109.flame_ref.refs_6_.refs_2_.refs_5_), custom_call_target="tpu_custom_call" | custom-call | tf_op jit(solution)/shard_map/pallas_call | solution.py:407
  82.3 2.2 %shard_map.113.refs_3_ = f32[64,8,128]{2,1,0:T(8,128)S(1)} custom-call(s32[4]{0:T(128)S(1)} %copy-done.5, f32[32,128]{1,0:T(8,128)S(1)} %get-tuple-element.28.coef_ref, f32[8,4,16,1024]{3,2,1,0:T(8,128)S(1)} %shard_map.110.own_ref, f32[6,4,16,1024]{3,2,1,0:T(8,128)S(1)} %shard_map.111.cross_ref, f32[2,16,1024]{2,1,0:T(8,128)S(1)} %get-tuple-element.59.refs_0_.refs_8_, ...), custom_call_target="tpu_custom_call" | custom-call | tf_op jit(solution)/shard_map/pallas_call | solution.py:407
  85.6 2.1 %shard_map.115 = (f32[2,16,1024]{2,1,0:T(8,128)S(1)}, f32[2,16,1024]{2,1,0:T(8,128)S(1)}, f32[2,16,1024]{2,1,0:T(8,128)S(1)}, f32[2,16,1024]{2,1,0:T(8,128)S(1)}...) custom-call(s32[4]{0:T(128)S(1)} %copy-done.5, ...), custom_call_target="tpu_custom_call" | custom-call | tf_op jit(solution)/shard_map/pallas_call | solution.py:407
  90.7 1.7 %collective-permute-start.27 = (f32[2,16,1024]{2,1,0:T(8,128)S(1)}, f32[2,16,1024]{2,1,0:T(8,128)S(1)}, u32[]{:S(2)}, u32[]{:S(2)}) collective-permute-start(f32[2,16,1024]{2,1,0:T(8,128)S(1)} %get-tuple-element.47), channel_id=1, source_target_pairs={{0,8},{2,10},{4,12},{6,14},{8,0},{10,2},{12,4},{14,6},{16,24},{18,... | collective-permute-start | bytes 393224 | tf_op jit(solution)/shard_map/ppermute | solution.py:437
  92.7 2.6 %collective-permute-start.29 = (f32[2,16,1024]{2,1,0:T(8,128)S(1)}, f32[2,16,1024]{2,1,0:T(8,128)S(1)}, u32[]{:S(2)}, u32[]{:S(2)}) collective-permute-start(f32[2,16,1024]{2,1,0:T(8,128)S(1)} %get-tuple-element.49), channel_id=1, source_target_pairs={{0,12},{2,14},{4,8},{6,10},{8,4},{10,6},{12,0},{14,2},{16,28},{18,... | collective-permute-start | bytes 393224 | tf_op jit(solution)/shard_map/ppermute | solution.py:437
  96.8 10.8 %all_to_all.5.refs_8_ = f32[16,8,128]{2,1,0:T(8,128)S(1)} all-to-all(f32[16,8,128]{2,1,0:T(8,128)S(1)} %bitcast.42), channel_id=1, replica_groups={{0,1,2,3,4,5,6,7,8,9,10,11,12,13,14,15},{16,17,18,19,20,21,22,23,24,25,..., dimensions={0} | all-to-all | bytes 131072 | tf_op jit(solution)/shard_map/all_to_all | solution.py:533
  (71 shorter events, 23.8 us)
Async XLA Ops:
  2.5 14.3 %collective-permute-start.10 = (f32[2,16,1024]{2,1,0:T(8,128)}, f32[2,16,1024]{2,1,0:T(8,128)S(1)}, u32[]{:S(2)}, u32[]{:S(2)}) collective-permute-start(f32[2,16,1024]{2,1,0:T(8,128)} %get-tuple-element.41), channel_id=1, source_target_pairs={{0,16},{2,18},{4,20},{6,22},{8,24},{10,26},{12,28},{14,30},{16,0},... | collective-permute-start | bytes 393224 | tf_op jit(solution)/shard_map/ppermute | solution.py:437
  8.0 10.3 %collective-permute-start.23 = (f32[2,16,1024]{2,1,0:T(8,128)S(1)}, f32[2,16,1024]{2,1,0:T(8,128)S(1)}, u32[]{:S(2)}, u32[]{:S(2)}) collective-permute-start(f32[2,16,1024]{2,1,0:T(8,128)S(1)} %get-tuple-element.54), channel_id=1, source_target_pairs={{0,2},{2,0},{4,6},{6,4},{8,10},{10,8},{12,14},{14,12},{16,18},{18,... | collective-permute-start | bytes 393224 | tf_op jit(solution)/shard_map/ppermute | solution.py:437
  12.1 17.7 %collective-permute-start.5 = (f32[72,512]{1,0:T(8,128)S(1)}, f32[72,512]{1,0:T(8,128)S(1)}, u32[]{:S(2)}, u32[]{:S(2)}) collective-permute-start(f32[72,512]{1,0:T(8,128)S(1)} %get-tuple-element.31), channel_id=1, source_target_pairs={{0,6},{2,4},{4,2},{6,0},{8,14},{10,12},{12,10},{14,8},{16,22},{18,... | collective-permute-start | bytes 442376 | tf_op jit(solution)/shard_map/ppermute | solution.py:437
  12.8 18.7 %collective-permute-start.9 = (f32[72,512]{1,0:T(8,128)S(1)}, f32[72,512]{1,0:T(8,128)S(1)}, u32[]{:S(2)}, u32[]{:S(2)}) collective-permute-start(f32[72,512]{1,0:T(8,128)S(1)} %get-tuple-element.32), channel_id=1, source_target_pairs={{0,14},{2,12},{4,10},{6,8},{8,6},{10,4},{12,2},{14,0},{16,30},{18,... | collective-permute-start | bytes 442376 | tf_op jit(solution)/shard_map/ppermute | solution.py:437
  16.8 10.3 %collective-permute-start.21 = (f32[2,16,1024]{2,1,0:T(8,128)S(1)}, f32[2,16,1024]{2,1,0:T(8,128)S(1)}, u32[]{:S(2)}, u32[]{:S(2)}) collective-permute-start(f32[2,16,1024]{2,1,0:T(8,128)S(1)} %get-tuple-element.56), channel_id=1, source_target_pairs={{0,4},{2,6},{4,0},{6,2},{8,12},{10,14},{12,8},{14,10},{16,20},{18,... | collective-permute-start | bytes 393224 | tf_op jit(solution)/shard_map/ppermute | solution.py:437
  24.0 16.1 %collective-permute-start.13 = (f32[72,512]{1,0:T(8,128)S(1)}, f32[72,512]{1,0:T(8,128)S(1)}, u32[]{:S(2)}, u32[]{:S(2)}) collective-permute-start(f32[72,512]{1,0:T(8,128)S(1)} %get-tuple-element.36), channel_id=1, source_target_pairs={{0,18},{2,16},{4,22},{6,20},{8,26},{10,24},{12,30},{14,28},{16,2},... | collective-permute-start | bytes 442376 | tf_op jit(solution)/shard_map/ppermute | solution.py:437
  27.1 14.6 %collective-permute-start.3 = (f32[72,512]{1,0:T(8,128)S(1)}, f32[72,512]{1,0:T(8,128)S(1)}, u32[]{:S(2)}, u32[]{:S(2)}) collective-permute-start(f32[72,512]{1,0:T(8,128)S(1)} %get-tuple-element.36), channel_id=1, source_target_pairs={{0,2},{2,0},{4,6},{6,4},{8,10},{10,8},{12,14},{14,12},{16,18},{18,... | collective-permute-start | bytes 442376 | tf_op jit(solution)/shard_map/ppermute | solution.py:437
  27.2 18.2 %collective-permute-start.15 = (f32[72,512]{1,0:T(8,128)S(1)}, f32[72,512]{1,0:T(8,128)S(1)}, u32[]{:S(2)}, u32[]{:S(2)}) collective-permute-start(f32[72,512]{1,0:T(8,128)S(1)} %get-tuple-element.37), channel_id=1, source_target_pairs={{0,20},{2,22},{4,16},{6,18},{8,28},{10,30},{12,24},{14,26},{16,4},... | collective-permute-start | bytes 442376 | tf_op jit(solution)/shard_map/ppermute | solution.py:437
  29.8 15.5 %collective-permute-start.4 = (f32[72,512]{1,0:T(8,128)S(1)}, f32[72,512]{1,0:T(8,128)S(1)}, u32[]{:S(2)}, u32[]{:S(2)}) collective-permute-start(f32[72,512]{1,0:T(8,128)S(1)} %get-tuple-element.37), channel_id=1, source_target_pairs={{0,4},{2,6},{4,0},{6,2},{8,12},{10,14},{12,8},{14,10},{16,20},{18,... | collective-permute-start | bytes 442376 | tf_op jit(solution)/shard_map/ppermute | solution.py:437
  31.4 17.1 %collective-permute-start.12 = (f32[72,512]{1,0:T(8,128)S(1)}, f32[72,512]{1,0:T(8,128)S(1)}, u32[]{:S(2)}, u32[]{:S(2)}) collective-permute-start(f32[72,512]{1,0:T(8,128)S(1)} %get-tuple-element.38), channel_id=1, source_target_pairs={{0,24},{2,26},{4,28},{6,30},{8,16},{10,18},{12,20},{14,22},{16,8},... | collective-permute-start | bytes 442376 | tf_op jit(solution)/shard_map/ppermute | solution.py:437
  40.1 11.8 %collective-permute-start.6 = (f32[72,512]{1,0:T(8,128)S(1)}, f32[72,512]{1,0:T(8,128)S(1)}, u32[]{:S(2)}, u32[]{:S(2)}) collective-permute-start(f32[72,512]{1,0:T(8,128)S(1)} %get-tuple-element.38), channel_id=1, source_target_pairs={{0,8},{2,10},{4,12},{6,14},{8,0},{10,2},{12,4},{14,6},{16,24},{18,... | collective-permute-start | bytes 442376 | tf_op jit(solution)/shard_map/ppermute | solution.py:437
  41.7 10.8 %collective-permute-start.14 = (f32[72,512]{1,0:T(8,128)S(1)}, f32[72,512]{1,0:T(8,128)S(1)}, u32[]{:S(2)}, u32[]{:S(2)}) collective-permute-start(f32[72,512]{1,0:T(8,128)S(1)} %get-tuple-element.39), channel_id=1, source_target_pairs={{0,26},{2,24},{4,30},{6,28},{8,18},{10,16},{12,22},{14,20},{16,10}... | collective-permute-start | bytes 442376 | tf_op jit(solution)/shard_map/ppermute | solution.py:437
  45.4 15.2 %collective-permute-start.16 = (f32[72,512]{1,0:T(8,128)S(1)}, f32[72,512]{1,0:T(8,128)S(1)}, u32[]{:S(2)}, u32[]{:S(2)}) collective-permute-start(f32[72,512]{1,0:T(8,128)S(1)} %get-tuple-element.40), channel_id=1, source_target_pairs={{0,28},{2,30},{4,24},{6,26},{8,20},{10,22},{12,16},{14,18},{16,12}... | collective-permute-start | bytes 442376 | tf_op jit(solution)/shard_map/ppermute | solution.py:437
  48.6 21.1 %collective-permute-start.8 = (f32[72,512]{1,0:T(8,128)S(1)}, f32[72,512]{1,0:T(8,128)S(1)}, u32[]{:S(2)}, u32[]{:S(2)}) collective-permute-start(f32[72,512]{1,0:T(8,128)S(1)} %get-tuple-element.40), channel_id=1, source_target_pairs={{0,12},{2,14},{4,8},{6,10},{8,4},{10,6},{12,0},{14,2},{16,28},{18,... | collective-permute-start | bytes 442376 | tf_op jit(solution)/shard_map/ppermute | solution.py:437
  51.8 33.8 %collective-permute-start.1 = (f32[72,512]{1,0:T(8,128)S(1)}, f32[72,512]{1,0:T(8,128)S(1)}, u32[]{:S(2)}, u32[]{:S(2)}) collective-permute-start(f32[72,512]{1,0:T(8,128)S(1)} %get-tuple-element.31), channel_id=1, source_target_pairs={{0,22},{2,20},{4,18},{6,16},{8,30},{10,28},{12,26},{14,24},{16,6},... | collective-permute-start | bytes 442376 | tf_op jit(solution)/shard_map/ppermute | solution.py:437
  52.5 33.1 %collective-permute-start.2 = (f32[72,512]{1,0:T(8,128)S(1)}, f32[72,512]{1,0:T(8,128)S(1)}, u32[]{:S(2)}, u32[]{:S(2)}) collective-permute-start(f32[72,512]{1,0:T(8,128)S(1)} %get-tuple-element.32), channel_id=1, source_target_pairs={{0,30},{2,28},{4,26},{6,24},{8,22},{10,20},{12,18},{14,16},{16,14}... | collective-permute-start | bytes 442376 | tf_op jit(solution)/shard_map/ppermute | solution.py:437
  54.9 27.4 %collective-permute-start.19 = (f32[2,16,1024]{2,1,0:T(8,128)S(1)}, f32[2,16,1024]{2,1,0:T(8,128)S(1)}, u32[]{:S(2)}, u32[]{:S(2)}) collective-permute-start(f32[2,16,1024]{2,1,0:T(8,128)S(1)} %get-tuple-element.58), channel_id=1, source_target_pairs={{0,12},{2,14},{4,8},{6,10},{8,4},{10,6},{12,0},{14,2},{16,28},{18,... | collective-permute-start | bytes 393224 | tf_op jit(solution)/shard_map/ppermute | solution.py:437
  60.6 23.9 %collective-permute-start.18 = (f32[2,16,1024]{2,1,0:T(8,128)S(1)}, f32[2,16,1024]{2,1,0:T(8,128)S(1)}, u32[]{:S(2)}, u32[]{:S(2)}) collective-permute-start(f32[2,16,1024]{2,1,0:T(8,128)S(1)} %get-tuple-element.60), channel_id=1, source_target_pairs={{0,10},{2,8},{4,14},{6,12},{8,2},{10,0},{12,6},{14,4},{16,26},{18,... | collective-permute-start | bytes 393224 | tf_op jit(solution)/shard_map/ppermute | solution.py:437
  69.7 14.8 %collective-permute-start.17 = (f32[2,16,1024]{2,1,0:T(8,128)S(1)}, f32[2,16,1024]{2,1,0:T(8,128)S(1)}, u32[]{:S(2)}, u32[]{:S(2)}) collective-permute-start(f32[2,16,1024]{2,1,0:T(8,128)S(1)} %get-tuple-element.61), channel_id=1, source_target_pairs={{0,14},{2,12},{4,10},{6,8},{8,6},{10,4},{12,2},{14,0},{16,30},{18,... | collective-permute-start | bytes 393224 | tf_op jit(solution)/shard_map/ppermute | solution.py:437
  90.7 17.0 %collective-permute-start.26 = (f32[2,16,1024]{2,1,0:T(8,128)S(1)}, f32[2,16,1024]{2,1,0:T(8,128)S(1)}, u32[]{:S(2)}, u32[]{:S(2)}) collective-permute-start(f32[2,16,1024]{2,1,0:T(8,128)S(1)} %get-tuple-element.46), channel_id=1, source_target_pairs={{0,6},{2,4},{4,2},{6,0},{8,14},{10,12},{12,10},{14,8},{16,22},{18,... | collective-permute-start | bytes 393224 | tf_op jit(solution)/shard_map/ppermute | solution.py:437
  90.7 17.0 %collective-permute-start.27 = (f32[2,16,1024]{2,1,0:T(8,128)S(1)}, f32[2,16,1024]{2,1,0:T(8,128)S(1)}, u32[]{:S(2)}, u32[]{:S(2)}) collective-permute-start(f32[2,16,1024]{2,1,0:T(8,128)S(1)} %get-tuple-element.47), channel_id=1, source_target_pairs={{0,8},{2,10},{4,12},{6,14},{8,0},{10,2},{12,4},{14,6},{16,24},{18,... | collective-permute-start | bytes 393224 | tf_op jit(solution)/shard_map/ppermute | solution.py:437
  92.4 15.2 %collective-permute-start.28 = (f32[2,16,1024]{2,1,0:T(8,128)S(1)}, f32[2,16,1024]{2,1,0:T(8,128)S(1)}, u32[]{:S(2)}, u32[]{:S(2)}) collective-permute-start(f32[2,16,1024]{2,1,0:T(8,128)S(1)} %get-tuple-element.48), channel_id=1, source_target_pairs={{0,10},{2,8},{4,14},{6,12},{8,2},{10,0},{12,6},{14,4},{16,26},{18,... | collective-permute-start | bytes 393224 | tf_op jit(solution)/shard_map/ppermute | solution.py:437
  92.7 15.0 %collective-permute-start.29 = (f32[2,16,1024]{2,1,0:T(8,128)S(1)}, f32[2,16,1024]{2,1,0:T(8,128)S(1)}, u32[]{:S(2)}, u32[]{:S(2)}) collective-permute-start(f32[2,16,1024]{2,1,0:T(8,128)S(1)} %get-tuple-element.49), channel_id=1, source_target_pairs={{0,12},{2,14},{4,8},{6,10},{8,4},{10,6},{12,0},{14,2},{16,28},{18,... | collective-permute-start | bytes 393224 | tf_op jit(solution)/shard_map/ppermute | solution.py:437
  95.6 12.1 %collective-permute-start.30 = (f32[2,16,1024]{2,1,0:T(8,128)S(1)}, f32[2,16,1024]{2,1,0:T(8,128)S(1)}, u32[]{:S(2)}, u32[]{:S(2)}) collective-permute-start(f32[2,16,1024]{2,1,0:T(8,128)S(1)} %get-tuple-element.50), channel_id=1, source_target_pairs={{0,14},{2,12},{4,10},{6,8},{8,6},{10,4},{12,2},{14,0},{16,30},{18,... | collective-permute-start | bytes 393224 | tf_op jit(solution)/shard_map/ppermute | solution.py:437
  (16 other events, 79.9 us)
